TPU v7x, 256 devices: a whole 4x4x8 slice. The times are simulated.
256 devices in a mesh: segment: 4 (over x), expert: 32 (over z, y), dp: 2 (over core).
Axes of the slice: x: 4, y: 4, z: 8, core: 2. Of those that a mesh axis runs over, the one named last changes fastest.
Arguments:
- entering: bfloat16 [4, 4096, 2560], P('segment', ('expert', 'dp')), may hold values from -0.59765625 to 0.59765625
- fresh: bfloat16 [1, 4096, 2560], P(None, ('expert', 'dp')), may hold values from -0.59765625 to 0.59765625
- w_gate: bfloat16 [4, 64, 2560, 768], P('segment', ('expert', 'dp')), may hold values from -0.125 to 0.125
- w_up: bfloat16 [4, 64, 2560, 768], P('segment', ('expert', 'dp')), may hold values from -0.125 to 0.125
- w_down: bfloat16 [4, 64, 768, 2560], P('segment', ('expert', 'dp')), may hold values from -0.21875 to 0.21875
- router: bfloat16 [4, 2560, 64], P('segment'), may hold values from -0.0625 to 0.0625
- gain: float32 [4, 2560], P('segment'), may hold values from 0.5 to 2
- routes: int32 [4, 2, 4096, 6], P('segment', None, ('expert', 'dp')), may hold values from 0 to 63, all different within a row; in each aligned block of 64 rows (0 to 63, 64 to 127, ..., all dimensions but the last counted through in order) at most 8 rows name the same one
Outputs:
- section_out: bfloat16 [4, 2, 4096, 2560], P('segment', None, ('expert', 'dp'))
Inputs may be any that keep to these rules, and one draw needn't show every extreme that they name: `routes`: in every aligned block of 64 rows (the tokens of one device for one section and micro-batch) no expert is named by more than 8 rows, and in some blocks one expert is named by exactly 8 rows; a row names 6 different experts.
All inputs are finite; a program needn't handle non-finite values.
Results may differ from a plain program's by a relative error of at most 0.009.
Values may be sent and summed in bfloat16 or wider, within the bound.
No kernel may reach another device: no remote copies, remote signals or barrier semaphores. Data moves between devices by JAX's collectives and lax.ppermute only.
A program may use at most 64 MiB of HBM per device.

v0:
```python
import jax
import jax.numpy as jnp
from jax import lax
from jax.sharding import PartitionSpec as P


def shifted(value, axis, steps):
    count = lax.axis_size(axis)
    leading, last = (max(0, -steps), min(count, count - steps))
    return lax.ppermute(value, axis, [(source, source + steps) for source in range(leading, last)])


def expert_rows(slot_rows, gate_weight, up_weight, down_weight):
    model_width = slot_rows.shape[-1]
    flattened = slot_rows.reshape(-1, model_width)
    gate_out = jnp.dot(flattened, gate_weight, preferred_element_type=jnp.float32)
    upper = jnp.dot(flattened, up_weight, preferred_element_type=jnp.float32)
    hidden = (jax.nn.silu(gate_out) * upper).astype(jnp.bfloat16)
    projected = jnp.dot(hidden, down_weight, preferred_element_type=jnp.float32).astype(
        jnp.bfloat16
    )
    return projected.reshape(slot_rows.shape)


def routed_slots(chosen_ids, expert_count):
    onehot = (chosen_ids[:, None] == jnp.arange(expert_count, dtype=jnp.int32)[None, :]).astype(
        jnp.int32
    )
    before = jnp.cumsum(onehot, axis=0) - onehot
    return jnp.sum(before * onehot, axis=1)


def section(incoming, gate_weight, up_weight, down_weight, router_layer, gain_layer, chosen_ids):
    tok_rows, model_width = incoming.shape
    top_count = chosen_ids.shape[1]
    experts = router_layer.shape[1]
    capacity = 4 * tok_rows * top_count // (3 * experts)
    values = incoming.astype(jnp.float32)
    inv_scale = lax.rsqrt(jnp.mean(values * values, axis=1, keepdims=True) + 1e-06)
    normed = (values * inv_scale * gain_layer[None, :]).astype(jnp.bfloat16)
    logits = jnp.dot(normed, router_layer, preferred_element_type=jnp.float32)
    scores = jax.nn.sigmoid(logits)
    chosen = jnp.take_along_axis(scores, chosen_ids, axis=1)
    mixing = chosen / jnp.sum(chosen, axis=1, keepdims=True)
    flat_picks = chosen_ids.reshape(-1)
    slot_ids = routed_slots(flat_picks, experts)
    owners = jnp.arange(tok_rows * top_count, dtype=jnp.int32) // top_count
    source = jnp.full((experts, capacity), tok_rows, jnp.int32).at[flat_picks, slot_ids].set(owners)
    padded = jnp.concatenate([normed, jnp.zeros((1, model_width), jnp.bfloat16)], axis=0)
    outgoing = padded[source]
    processed = expert_rows(
        lax.all_to_all(outgoing, ("expert", "dp"), split_axis=0, concat_axis=0, tiled=True),
        gate_weight,
        up_weight,
        down_weight,
    )
    returned = lax.all_to_all(processed, ("expert", "dp"), split_axis=0, concat_axis=0, tiled=True)
    landed = returned[flat_picks, slot_ids].reshape(tok_rows, top_count, model_width)
    summed = values + jnp.sum(landed.astype(jnp.float32) * mixing[:, :, None], axis=1)
    return summed.astype(jnp.bfloat16)


def shards(entering, fresh, w_gate, w_up, w_down, router, gain, routes):
    segment_id = lax.axis_index("segment")
    micro_count = routes.shape[1]
    current = entering[0]
    results = []
    for step_index in range(micro_count):
        if step_index > 0:
            arrived = shifted(results[-1], "segment", 1)
            current = jnp.where(segment_id == 0, fresh[step_index - 1], arrived)
        output = section(
            current,
            w_gate[0, 0],
            w_up[0, 0],
            w_down[0, 0],
            router[0],
            gain[0],
            routes[0, step_index],
        )
        results.append(output)
    return jnp.stack(results)[None]


def solution(mesh):
    in_specs = (
        P("segment", ("expert", "dp"), None),
        P(None, ("expert", "dp"), None),
        P("segment", ("expert", "dp"), None, None),
        P("segment", ("expert", "dp"), None, None),
        P("segment", ("expert", "dp"), None, None),
        P("segment", None, None),
        P("segment", None),
        P("segment", None, ("expert", "dp"), None),
    )
    out_specs = P("segment", None, ("expert", "dp"), None)
    return jax.shard_map(shards, mesh=mesh, in_specs=in_specs, out_specs=out_specs, check_vma=False)
```

profile of v0, /device:TPU:7, one launch (start us, length us, event | category | flops | bytes accessed | tf_op | source)
XLA Modules:
  0.0 393.5 jit_solution(3504204603303843737)
XLA Ops:
  1.8 1.1 fusion.43
  3.0 0.9 reduce-window.14
  4.2 0.9 reduce-window.16
  5.7 18.2 %scatter_fusion = s32[64,8]{0,1:T(8,128)S(1)} fusion(s32[64,8]{0,1:T(8,128)S(1)} %broadcast.157.clone, s32[384]{0:T(512)S(1)} %get-tuple-element.14, s32[384]{0:T(512)S(1)} %add_select_fusion), kind=kCustom, calls=%fused_computation.6 | custom fusion | bytes 7680 | tf_op jit(solution)/shard_map/scatter | solution.py:48
  24.4 2.6 gather_fusion
  27.0 75.1 %all_to_all.20 = bf16[64,8,2560]{2,1,0:T(8,128)(2,1)S(1)} all-to-all(bf16[64,8,2560]{2,1,0:T(8,128)(2,1)S(1)} %bitcast.167), channel_id=1, replica_groups=mesh['segment'=4,'expert'=32,'dp'=2] {'expert','dp'}, dimensions={0} | all-to-all | bytes 5242880 | tf_op jit(solution)/shard_map/all_to_all | solution.py:52
  102.1 1.5 copy-done.8
  103.6 2.2 fusion.10
  105.8 11.2 %fusion = bf16[64,8,2560]{2,1,0:T(8,128)(2,1)} fusion(bf16[1,1,768,2560]{3,2,1,0:T(8,128)(2,1)} %param.14, f32[512,768]{1,0:T(8,128)S(1)} %fusion.10, bf16[1,1,2560,768]{3,2,1,0:T(8,128)(2,1)} %param.13, bf16[64,8,2560]{2,1,0:T(8,128)(2,1)} %copy-done.8), kind=kOutput, calls=%fused_computation.12 | convolution fusion | flops 4030201856 | bytes 14680064 | tf_op jit(solution)/shard_map/dot_general | solution.py:19
  117.0 5.8 %all-to-all-start.1 = ((bf16[64,8,2560]{2,1,0:T(8,128)(2,1)}), bf16[64,8,2560]{2,1,0:T(8,128)(2,1)S(1)}, u32[]{:S(2)}, u32[]{:S(2)}) async-start(bf16[64,8,2560]{2,1,0:T(8,128)(2,1)} %fusion), calls=%async_computation.1 | async-start | bytes 5242880 | tf_op jit(solution)/shard_map/all_to_all | solution.py:57
  123.4 2.9 gather_fusion.4
  126.7 18.2 %scatter_fusion.1 = s32[64,8]{0,1:T(8,128)S(1)} fusion(s32[64,8]{0,1:T(8,128)S(1)} %broadcast.157.clone.1, s32[384]{0:T(512)S(1)} %get-tuple-element.7, s32[384]{0:T(512)S(1)} %add_select_fusion), kind=kCustom, calls=%fused_computation.7 | custom fusion | bytes 7680 | tf_op jit(solution)/shard_map/scatter | solution.py:48
  144.9 38.9 %all-to-all-done.1 = bf16[64,8,2560]{2,1,0:T(8,128)(2,1)S(1)} async-done(((bf16[64,8,2560]{2,1,0:T(8,128)(2,1)}), bf16[64,8,2560]{2,1,0:T(8,128)(2,1)S(1)}, u32[]{:S(2)}, u32[]{:S(2)}) %all-to-all-start.1) | async-done | bytes 2621472 | tf_op jit(solution)/shard_map/all_to_all | solution.py:57
  183.8 11.4 %gather_fusion.1 = bf16[384,2560]{1,0:T(8,128)(2,1)} fusion(bf16[64,8,2560]{2,1,0:T(8,128)(2,1)S(1)} %all-to-all-done.1, s32[384]{0:T(512)S(1)} %get-tuple-element.15), kind=kCustom, calls=%fused_computation.3 | custom fusion | bytes 3935232 | tf_op jit(solution)/shard_map/gather | solution.py:58
  195.2 4.5 %reshape.187 = f32[64,6,2560]{2,1,0:T(8,128)} reshape(bf16[384,2560]{1,0:T(8,128)(2,1)} %gather_fusion.1) | data formatting | bytes 5898240 | tf_op jit(solution)/shard_map/convert_element_type | solution.py:59
  199.7 4.4 %multiply_reduce_fusion.1 = f32[64,2560]{1,0:T(8,128)S(1)} fusion(f32[64,6,2560]{2,1,0:T(8,128)} %reshape.187, f32[64,6]{1,0:T(8,128)S(1)} %copy.19), kind=kLoop, calls=%fused_computation.9 | loop fusion | flops 1802240 | bytes 4589056 | tf_op jit(solution)/shard_map/reduce_sum | solution.py:59
  205.0 1.3 collective-permute-start
  206.5 7.6 %collective-permute-done = bf16[64,2560]{1,0:T(8,128)(2,1)S(1)} collective-permute-done((bf16[64,2560]{1,0:T(8,128)(2,1)S(1)}, bf16[64,2560]{1,0:T(8,128)(2,1)S(1)}, u32[]{:S(2)}, u32[]{:S(2)}) %collective-permute-start) | collective-permute-done | bytes 327712 | tf_op jit(solution)/shard_map/ppermute | solution.py:10
  215.8 2.6 gather_fusion.2
  218.5 72.0 %all_to_all.21 = bf16[64,8,2560]{2,1,0:T(8,128)(2,1)S(1)} all-to-all(bf16[64,8,2560]{2,1,0:T(8,128)(2,1)S(1)} %bitcast.168), channel_id=1, replica_groups=mesh['segment'=4,'expert'=32,'dp'=2] {'expert','dp'}, dimensions={0} | all-to-all | bytes 5242880 | tf_op jit(solution)/shard_map/all_to_all | solution.py:52
  290.5 1.5 copy-done.9
  292.0 2.2 fusion.8
  294.2 11.2 %fusion.1 = bf16[64,8,2560]{2,1,0:T(8,128)(2,1)} fusion(bf16[1,1,768,2560]{3,2,1,0:T(8,128)(2,1)} %param.14, f32[512,768]{1,0:T(8,128)S(1)} %fusion.8, bf16[1,1,2560,768]{3,2,1,0:T(8,128)(2,1)} %param.13, bf16[64,8,2560]{2,1,0:T(8,128)(2,1)} %copy-done.9), kind=kOutput, calls=%fused_computation.13 | convolution fusion | flops 4030201856 | bytes 14680064 | tf_op jit(solution)/shard_map/dot_general | solution.py:19
  305.4 5.8 %all-to-all-start.3 = ((bf16[64,8,2560]{2,1,0:T(8,128)(2,1)}), bf16[64,8,2560]{2,1,0:T(8,128)(2,1)S(1)}, u32[]{:S(2)}, u32[]{:S(2)}) async-start(bf16[64,8,2560]{2,1,0:T(8,128)(2,1)} %fusion.1), calls=%async_computation.3 | async-start | bytes 5242880 | tf_op jit(solution)/shard_map/all_to_all | solution.py:57
  311.4 1.9 fusion.49
  313.3 1.2 fusion.26
  314.5 2.9 gather_fusion.5
  317.8 54.5 %all-to-all-done.3 = bf16[64,8,2560]{2,1,0:T(8,128)(2,1)S(1)} async-done(((bf16[64,8,2560]{2,1,0:T(8,128)(2,1)}), bf16[64,8,2560]{2,1,0:T(8,128)(2,1)S(1)}, u32[]{:S(2)}, u32[]{:S(2)}) %all-to-all-start.3) | async-done | bytes 2621472 | tf_op jit(solution)/shard_map/all_to_all | solution.py:57
  372.2 11.4 %gather_fusion.3 = bf16[384,2560]{1,0:T(8,128)(2,1)} fusion(bf16[64,8,2560]{2,1,0:T(8,128)(2,1)S(1)} %all-to-all-done.3, s32[384]{0:T(512)S(1)} %get-tuple-element.6), kind=kCustom, calls=%fused_computation.5 | custom fusion | bytes 3935232 | tf_op jit(solution)/shard_map/gather | solution.py:58
  383.6 4.5 %reshape.188 = f32[64,6,2560]{2,1,0:T(8,128)} reshape(bf16[384,2560]{1,0:T(8,128)(2,1)} %gather_fusion.3) | data formatting | bytes 5898240 | tf_op jit(solution)/shard_map/convert_element_type | solution.py:59
  388.1 4.5 %multiply_reduce_fusion = f32[64,2560]{1,0:T(8,128)S(1)} fusion(f32[64,6,2560]{2,1,0:T(8,128)} %reshape.188, f32[64,6]{1,0:T(8,128)S(1)} %copy.28), kind=kLoop, calls=%fused_computation.8 | loop fusion | flops 1802240 | bytes 4589056 | tf_op jit(solution)/shard_map/reduce_sum | solution.py:59
  392.6 0.9 maximum_bitcast_fusion
  (83 shorter events, 7.3 us)
Async XLA Ops:
  0.0 123.1 %copy-start = (bf16[1,2560,64]{1,2,0:T(8,128)(2,1)S(1)}, bf16[1,2560,64]{1,2,0:T(8,128)(2,1)}, u32[]{:S(2)}) copy-start(bf16[1,2560,64]{1,2,0:T(8,128)(2,1)} %param.15) | copy-start | bytes 983044
  3.9 20.2 %copy-start.12 = (f32[1,2560]{1,0:T(1,128)S(1)}, f32[1,2560]{1,0:T(1,128)}, u32[]{:S(2)}) copy-start(f32[1,2560]{1,0:T(1,128)} %param.16) | copy-start | bytes 30724
  3.9 20.2 %copy-start.2 = (bf16[1,64,2560]{2,1,0:T(8,128)(2,1)S(1)}, bf16[1,64,2560]{2,1,0:T(8,128)(2,1)}, u32[]{:S(2)}) copy-start(bf16[1,64,2560]{2,1,0:T(8,128)(2,1)} %param.10) | copy-start | bytes 983044
  27.0 76.6 %copy-start.13 = (bf16[1,1,2560,768]{3,2,1,0:T(8,128)(2,1)S(1)}, bf16[1,1,2560,768]{3,2,1,0:T(8,128)(2,1)}, u32[]{:S(2)}) copy-start(bf16[1,1,2560,768]{3,2,1,0:T(8,128)(2,1)} %param.12) | copy-start | bytes 11796484
  102.1 1.5 copy-start.8
  117.0 6.1 %copy-start.3 = (bf16[1,64,2560]{2,1,0:T(8,128)(2,1)S(1)}, bf16[1,64,2560]{2,1,0:T(8,128)(2,1)}, u32[]{:S(2)}) copy-start(bf16[1,64,2560]{2,1,0:T(8,128)(2,1)} %param.10) | copy-start | bytes 983044
  117.0 66.8 %all-to-all-start.1 = ((bf16[64,8,2560]{2,1,0:T(8,128)(2,1)}), bf16[64,8,2560]{2,1,0:T(8,128)(2,1)S(1)}, u32[]{:S(2)}, u32[]{:S(2)}) async-start(bf16[64,8,2560]{2,1,0:T(8,128)(2,1)} %fusion), calls=%async_computation.1 | async-start | bytes 5242880 | tf_op jit(solution)/shard_map/all_to_all | solution.py:57
  199.7 14.4 %copy-start.11 = (bf16[1,64,2560]{2,1,0:T(8,128)(2,1)S(1)}, bf16[1,64,2560]{2,1,0:T(8,128)(2,1)}, u32[]{:S(2)}) copy-start(bf16[1,64,2560]{2,1,0:T(8,128)(2,1)} %param.11) | copy-start | bytes 983044
  204.1 0.8 copy-start.1
  205.0 9.1 %collective-permute-start = (bf16[64,2560]{1,0:T(8,128)(2,1)S(1)}, bf16[64,2560]{1,0:T(8,128)(2,1)S(1)}, u32[]{:S(2)}, u32[]{:S(2)}) collective-permute-start(bf16[64,2560]{1,0:T(8,128)(2,1)S(1)} %fusion.46), channel_id=1, source_target_pairs={{0,64},{64,128},{128,192},{1,65},{65,129},{129,193},{2,66},{66,130... | collective-permute-start | bytes 983048 | tf_op jit(solution)/shard_map/ppermute | solution.py:10
  214.3 0.7 copy-start.5
  215.1 0.7 copy-start.7
  218.5 73.5 %copy-start.14 = (bf16[1,1,2560,768]{3,2,1,0:T(8,128)(2,1)S(1)}, bf16[1,1,2560,768]{3,2,1,0:T(8,128)(2,1)}, u32[]{:S(2)}) copy-start(bf16[1,1,2560,768]{3,2,1,0:T(8,128)(2,1)} %param.12) | copy-start | bytes 11796484
  290.5 1.5 copy-start.9
  305.4 6.1 %copy-start.4 = (bf16[1,64,2560]{2,1,0:T(8,128)(2,1)S(1)}, bf16[1,64,2560]{2,1,0:T(8,128)(2,1)}, u32[]{:S(2)}) copy-start(bf16[1,64,2560]{2,1,0:T(8,128)(2,1)} %param.10) | copy-start | bytes 983044
  305.4 66.9 %all-to-all-start.3 = ((bf16[64,8,2560]{2,1,0:T(8,128)(2,1)}), bf16[64,8,2560]{2,1,0:T(8,128)(2,1)S(1)}, u32[]{:S(2)}, u32[]{:S(2)}) async-start(bf16[64,8,2560]{2,1,0:T(8,128)(2,1)} %fusion.1), calls=%async_computation.3 | async-start | bytes 5242880 | tf_op jit(solution)/shard_map/all_to_all | solution.py:57
  388.1 4.5 %copy-start.6 = (bf16[64,2560]{1,0:T(8,128)(2,1)S(1)}, bf16[64,2560]{1,0:T(8,128)(2,1)}, u32[]{:S(2)}) copy-start(bf16[64,2560]{1,0:T(8,128)(2,1)} %copy-done.5) | copy-start | bytes 983044
  388.1 4.5 %copy-start.10 = (bf16[1,64,2560]{2,1,0:T(8,128)(2,1)S(1)}, bf16[1,64,2560]{2,1,0:T(8,128)(2,1)}, u32[]{:S(2)}) copy-start(bf16[1,64,2560]{2,1,0:T(8,128)(2,1)} %fusion.49) | copy-start | bytes 983044
where the time goes:
time: 395 us; the launch traced here: 394 us
  blocking collectives  147 us (37%)
  waiting for transfers between devices  101 us (26%)
  local copies, waits for them, and re-layouts  88.1 us (22%)
  matrix products  28.3 us (7%)
  other arithmetic  15.8 us (4%)
  starting transfers between devices  12.9 us (3%)
    all_to_all x2, blocking collectives, section(): lax.all_to_all(outgoing, ('expert', 'dp'), split_axis=0, concat_axis=0, t...  147 us
    all_to_all x2, waiting for transfers between devices, section(): lax.all_to_all(processed, ('expert', 'dp'), split_axis=0, concat_axis=0,...  93.4 us
    scatter x2, local copies, waits for them, and re-layouts, section(): jnp.full((experts, capacity), tok_rows, jnp.int32).at[flat_picks, slot_ids]  36.5 us
    gather x2, local copies, waits for them, and re-layouts, section(): returned[flat_picks, slot_ids].reshape(tok_rows, top_count, model_width)  22.7 us
    dot_general x2, matrix products, expert_rows(): jnp.dot(hidden, down_weight, preferred_element_type=jnp.float32)  22.4 us
    all_to_all x2, starting transfers between devices, section(): lax.all_to_all(processed, ('expert', 'dp'), split_axis=0, concat_axis=0,...  11.6 us
    convert_element_type x2, local copies, waits for them, and re-layouts, section(): landed.astype(jnp.float32) * mixing[:, :, None]  8.97 us
    reduce_sum x2, other arithmetic, section(): jnp.sum(landed.astype(jnp.float32) * mixing[:, :, None], axis=1)  8.9 us
  transfers between devices with their start and end apart: 3, of which 3 were waited for; matrix products, arithmetic and copies ran while one was open for 7% of the time, Pallas kernels for 0%

commit v1 on v0

v1 whole, which is shorter than its diff:
```python
import jax
import jax.numpy as jnp
from jax import lax
from jax.experimental import pallas as pl
from jax.experimental.pallas import tpu as pltpu
from jax.sharding import PartitionSpec as P

CAP = 8
GROUP = ("expert", "dp")


def dot(lhs, rhs, lhs_dim=1, rhs_dim=0):
    return lax.dot_general(
        lhs, rhs, (((lhs_dim,), (rhs_dim,)), ((), ())), preferred_element_type=jnp.float32
    )


def column_tiles(width, tile):
    return [slice(start, min(start + tile, width)) for start in range(0, width, tile)]


def prepare_kernel(first_ref, arrived_ref, fresh_ref, gain_ref, router_ref, picks_ref,
                   current_ref, rows_ref, weights_ref):
    tokens, width = current_ref.shape
    experts = router_ref.shape[0]
    picked = arrived_ref[...]
    current = jnp.where(first_ref[0] == 1, fresh_ref[...], picked)
    current_ref[...] = current
    values = current.astype(jnp.float32)
    inv_scale = lax.rsqrt(jnp.mean(values * values, axis=1, keepdims=True) + 1e-06)
    normed = (values * inv_scale * gain_ref[...]).astype(jnp.bfloat16)
    logits = dot(router_ref[...], normed, 1, 1)
    expert_ids = lax.broadcasted_iota(jnp.int32, (experts, tokens), 0)
    chosen = jnp.zeros((experts, tokens), jnp.float32)
    for choice in range(picks_ref.shape[0]):
        chosen = chosen + jnp.where(picks_ref[choice : choice + 1, :] == expert_ids, 1.0, 0.0)
    scores = chosen / (1.0 + jnp.exp(-logits))
    mixing = scores / jnp.sum(scores, axis=0, keepdims=True)
    before = jnp.where(
        lax.broadcasted_iota(jnp.int32, (tokens, tokens), 0)
        < lax.broadcasted_iota(jnp.int32, (tokens, tokens), 1), 1.0, 0.0
    ).astype(jnp.bfloat16)
    rank = dot(chosen.astype(jnp.bfloat16), before)
    slot = jnp.where(chosen > 0.0, rank, float(CAP))
    slot_rows = jnp.broadcast_to(slot[:, None, :], (experts, CAP, tokens))
    slot_ids = lax.broadcasted_iota(jnp.int32, (experts, CAP, tokens), 1).astype(jnp.float32)
    here = slot_rows == slot_ids
    pick = jnp.where(here, 1.0, 0.0).reshape(experts * CAP, tokens).astype(jnp.bfloat16)
    mixed = jnp.where(here, jnp.broadcast_to(mixing[:, None, :], here.shape), 0.0)
    weights_ref[...] = mixed.reshape(experts * CAP, tokens).astype(jnp.bfloat16)
    for cols in column_tiles(width, 512):
        rows_ref[:, cols] = dot(pick, normed[:, cols]).astype(jnp.bfloat16)


def prepare(first, arrived, fresh, gain, router, picks):
    tokens, width = arrived.shape
    slots = router.shape[0] * CAP
    vmem = pl.BlockSpec(memory_space=pltpu.VMEM)
    return pl.pallas_call(
        prepare_kernel,
        out_shape=(
            jax.ShapeDtypeStruct((tokens, width), jnp.bfloat16),
            jax.ShapeDtypeStruct((slots, width), jnp.bfloat16),
            jax.ShapeDtypeStruct((slots, tokens), jnp.bfloat16),
        ),
        in_specs=[pl.BlockSpec(memory_space=pltpu.SMEM)] + [vmem] * 5,
        out_specs=(vmem, vmem, vmem),
        name="prepare",
    )(first, arrived, fresh, gain, router, picks)


def experts_kernel(rows_ref, gate_ref, up_ref, down_ref, out_ref, total_ref):
    step = pl.program_id(0)
    rows = rows_ref[...]
    gate = dot(rows, gate_ref[...])
    up = dot(rows, up_ref[...])
    hidden = (gate / (1.0 + jnp.exp(-gate)) * up).astype(jnp.bfloat16)
    width = out_ref.shape[1]
    steps = pl.num_programs(0)

    @pl.when(step == 0)
    def _():
        for cols in column_tiles(width, 512):
            total_ref[:, cols] = dot(hidden, down_ref[:, cols])

    @pl.when((step > 0) & (step < steps - 1))
    def _():
        for cols in column_tiles(width, 512):
            total_ref[:, cols] += dot(hidden, down_ref[:, cols])

    @pl.when(step == steps - 1)
    def _():
        for cols in column_tiles(width, 512):
            out_ref[:, cols] = (total_ref[:, cols] + dot(hidden, down_ref[:, cols])).astype(jnp.bfloat16)


def run_experts(rows, w_gate, w_up, w_down):
    count, width = rows.shape
    hidden = w_gate.shape[1]
    tile = 256
    return pl.pallas_call(
        experts_kernel,
        out_shape=jax.ShapeDtypeStruct((count, width), jnp.bfloat16),
        grid_spec=pltpu.PrefetchScalarGridSpec(
            num_scalar_prefetch=0,
            grid=(hidden // tile,),
            in_specs=[
                pl.BlockSpec((count, width), lambda i: (0, 0)),
                pl.BlockSpec((width, tile), lambda i: (0, i)),
                pl.BlockSpec((width, tile), lambda i: (0, i)),
                pl.BlockSpec((tile, width), lambda i: (i, 0)),
            ],
            out_specs=pl.BlockSpec((count, width), lambda i: (0, 0)),
            scratch_shapes=[pltpu.VMEM((count, width), jnp.float32)],
        ),
        compiler_params=pltpu.CompilerParams(vmem_limit_bytes=40 << 20),
        name="experts",
    )(rows, w_gate, w_up, w_down)


def combine_kernel(current_ref, weights_ref, landed_ref, out_ref):
    weights = jnp.transpose(weights_ref[...])
    for cols in column_tiles(out_ref.shape[1], 512):
        total = current_ref[:, cols].astype(jnp.float32) + dot(weights, landed_ref[:, cols])
        out_ref[:, cols] = total.astype(jnp.bfloat16)


def combine(current, weights, landed):
    vmem = pl.BlockSpec(memory_space=pltpu.VMEM)
    return pl.pallas_call(
        combine_kernel,
        out_shape=jax.ShapeDtypeStruct(current.shape, jnp.bfloat16),
        in_specs=[vmem] * 3,
        out_specs=vmem,
        name="combine",
    )(current, weights, landed)


def exchange(rows):
    count, width = rows.shape
    parts = rows.reshape(count // CAP, CAP, width)
    moved = lax.all_to_all(parts, GROUP, split_axis=0, concat_axis=0, tiled=True)
    return moved.reshape(count, width)


def shards(entering, fresh, w_gate, w_up, w_down, router, gain, routes):
    at_start = (lax.axis_index("segment") == 0).astype(jnp.int32).reshape(1)
    never = jnp.zeros((1,), jnp.int32)
    router_rows = jnp.transpose(router[0])
    picks = jnp.transpose(routes[0], (0, 2, 1))
    results = []
    count = lax.axis_size("segment")
    for step in range(routes.shape[1]):
        if step == 0:
            first, arrived, other = never, entering[0], entering[0]
        else:
            arrived = lax.ppermute(results[-1], "segment", [(i, i + 1) for i in range(count - 1)])
            first, other = at_start, fresh[step - 1]
        current, rows, weights = prepare(first, arrived, other, gain, router_rows, picks[step])
        outputs = run_experts(exchange(rows), w_gate[0, 0], w_up[0, 0], w_down[0, 0])
        results.append(combine(current, weights, exchange(outputs)))
    return jnp.stack(results)[None]


def solution(mesh):
    tokens = P("segment", ("expert", "dp"), None)
    weights = P("segment", ("expert", "dp"), None, None)
    in_specs = (
        tokens, P(None, ("expert", "dp"), None), weights, weights, weights,
        P("segment", None, None), P("segment", None), P("segment", None, ("expert", "dp"), None),
    )
    out_specs = P("segment", None, ("expert", "dp"), None)
    return jax.shard_map(shards, mesh=mesh, in_specs=in_specs, out_specs=out_specs, check_vma=False)
```

time: 395 us -> 333 us (0.84)
  blocking collectives: 147 us -> 281 us
  waiting for transfers between devices: 101 us -> 9.75 us
  local copies, waits for them, and re-layouts: 88.1 us -> 6.26 us
  Pallas kernels: 0 us -> 32 us
  matrix products: 28.3 us -> 0 us
  other arithmetic: 15.8 us -> 1.87 us
  starting transfers between devices: 12.9 us -> 1.28 us
    all_to_all x2 -> x4, blocking collectives: 147 us -> 281 us  [exchange(): lax.all_to_all(parts, GROUP, split_axis=0, concat_axis=0, tiled=True)]
    all_to_all x2 -> x0, waiting for transfers between devices: 93.4 us -> none  [section(): lax.all_to_all(processed, ('expert', 'dp'), split_axis=0, concat_axis=0,...]
    scatter x2 -> x0, local copies, waits for them, and re-layouts: 36.5 us -> none  [section(): jnp.full((experts, capacity), tok_rows, jnp.int32).at[flat_picks, slot_ids]]
    gather x14 -> x0, local copies, waits for them, and re-layouts: 34.6 us -> none  [the longest x2 22.7 us: section(): returned[flat_picks, slot_ids].reshape(tok_rows, top_count, model_width)]
    pallas_call x0 -> x6, Pallas kernels: none -> 32 us  [the longest x2 17.8 us: run_experts(): pl.pallas_call(experts_kernel, out_shape=jax.ShapeDtypeStruct((count, wid...]
    dot_general x6 -> x0, matrix products: 28.3 us -> none  [the longest x2 22.4 us: expert_rows(): jnp.dot(hidden, down_weight, preferred_element_type=jnp.float32)]
    all_to_all x2 -> x0, starting transfers between devices: 11.6 us -> none  [section(): lax.all_to_all(processed, ('expert', 'dp'), split_axis=0, concat_axis=0,...]
    reduce_sum x8 -> x0, other arithmetic: 10.5 us -> none  [the longest x2 8.9 us: section(): jnp.sum(landed.astype(jnp.float32) * mixing[:, :, None], axis=1)]
  transfers between devices with their start and end apart: 3 -> 1, of which waited for: 3 -> 1; matrix products, arithmetic and copies ran while one was open for 7% -> 0% of each run, Pallas kernels for 0% -> 0%
where the time goes in v1:
time: 333 us; the launch traced here: 332 us
  blocking collectives  281 us (84%)
  Pallas kernels  32 us (10%)
  waiting for transfers between devices  9.75 us (3%)
  local copies, waits for them, and re-layouts  6.26 us (2%)
    all_to_all x4, blocking collectives, exchange(): lax.all_to_all(parts, GROUP, split_axis=0, concat_axis=0, tiled=True)  281 us
    pallas_call x2, Pallas kernels, run_experts(): pl.pallas_call(experts_kernel, out_shape=jax.ShapeDtypeStruct((count, wid...  17.8 us
    ppermute x1, waiting for transfers between devices, shards(): lax.ppermute(results[-1], 'segment', [(i, i + 1) for i in range(count - 1)])  9.75 us
    pallas_call x2, Pallas kernels, prepare(): pl.pallas_call(prepare_kernel, out_shape=(jax.ShapeDtypeStruct((tokens, w...  7.7 us
  transfers between devices with their start and end apart: 1, of which 1 were waited for; matrix products, arithmetic and copies ran while one was open for 0% of the time, Pallas kernels for 0%

profile of v1, /device:TPU:7, one launch (start us, length us, event | category | flops | bytes accessed | tf_op | source)
XLA Modules:
  0.0 332.1 jit_solution(4564721368337282876)
XLA Ops:
  0.0 0.7 copy.11
  0.7 0.6 slice_bitcast_fusion
  1.3 3.9 %prepare.2 = (bf16[64,2560]{1,0:T(8,128)(2,1)}, bf16[512,2560]{1,0:T(8,128)(2,1)}, bf16[512,64]{1,0:T(8,128)(2,1)}) custom-call(s32[1]{0:T(128)} %constant.2.clone.1.first_ref, bf16[64,2560]{1,0:T(8,128)(2,1)} %bitcast.44, bf16[64,2560]{1,0:T(8,128)(2,1)} %bitcast.45, f32[1,2560]{1,0:T(1,128)} %gain_ref.3, bf16[64,2560]{1,0:T(8,128)(2,1)} %bitcast.46, ...), custom_call_target="tpu_custom_call" | custom-call | tf_op jit(solution)/shard_map/prepare/pallas_call | solution.py:59
  5.2 0.0 copy-start
  5.2 75.3 %all_to_all.20 = bf16[64,8,2560]{2,1,0:T(8,128)(2,1)S(1)} all-to-all(bf16[64,8,2560]{2,1,0:T(8,128)(2,1)} %bitcast.43), channel_id=1, replica_groups=mesh['segment'=4,'expert'=32,'dp'=2] {'expert','dp'}, dimensions={0} | all-to-all | bytes 5242880 | tf_op jit(solution)/shard_map/all_to_all | solution.py:142
  80.5 0.0 copy-done
  80.5 0.0 copy-start.2
  80.5 2.1 copy-done.2
  82.6 8.9 %experts.2 = bf16[512,2560]{1,0:T(8,128)(2,1)S(1)} custom-call(bf16[512,2560]{1,0:T(8,128)(2,1)S(1)} %bitcast.34, bf16[2560,768]{1,0:T(8,128)(2,1)S(1)} %bitcast.30, bf16[2560,768]{1,0:T(8,128)(2,1)S(1)} %bitcast.32, bf16[768,2560]{1,0:T(8,128)(2,1)} %bitcast.38), custom_call_target="tpu_custom_call" | custom-call | tf_op jit(solution)/shard_map/experts/pallas_call | solution.py:101
  91.5 68.3 %all_to_all.21 = bf16[64,8,2560]{2,1,0:T(8,128)(2,1)} all-to-all(bf16[64,8,2560]{2,1,0:T(8,128)(2,1)S(1)} %bitcast.35), channel_id=1, replica_groups=mesh['segment'=4,'expert'=32,'dp'=2] {'expert','dp'}, dimensions={0} | all-to-all | bytes 5242880 | tf_op jit(solution)/shard_map/all_to_all | solution.py:142
  159.7 3.2 combine.2
  163.0 1.3 collective-permute-start
  164.3 9.7 %collective-permute-done.arrived_ref = bf16[64,2560]{1,0:T(8,128)(2,1)S(1)} collective-permute-done((bf16[64,2560]{1,0:T(8,128)(2,1)}, bf16[64,2560]{1,0:T(8,128)(2,1)S(1)}, u32[]{:S(2)}, u32[]{:S(2)}) %collective-permute-start) | collective-permute-done | bytes 327712 | tf_op jit(solution)/shard_map/ppermute | solution.py:157
  174.0 0.0 copy-start.5
  174.0 0.7 copy-done.5
  174.8 3.8 %prepare.3 = (bf16[64,2560]{1,0:T(8,128)(2,1)}, bf16[512,2560]{1,0:T(8,128)(2,1)}, bf16[512,64]{1,0:T(8,128)(2,1)}) custom-call(s32[1]{0:T(128)} %bitcast.14.first_ref, bf16[64,2560]{1,0:T(8,128)(2,1)} %copy-done.5, bf16[64,2560]{1,0:T(8,128)(2,1)} %bitcast.50, f32[1,2560]{1,0:T(1,128)} %gain_ref.3, bf16[64,2560]{1,0:T(8,128)(2,1)} %bitcast.47, ...), custom_call_target="tpu_custom_call" | custom-call | tf_op jit(solution)/shard_map/prepare/pallas_call | solution.py:59
  178.6 0.0 copy-start.1
  178.6 69.0 %all_to_all.22 = bf16[64,8,2560]{2,1,0:T(8,128)(2,1)S(1)} all-to-all(bf16[64,8,2560]{2,1,0:T(8,128)(2,1)} %bitcast.42), channel_id=1, replica_groups=mesh['segment'=4,'expert'=32,'dp'=2] {'expert','dp'}, dimensions={0} | all-to-all | bytes 5242880 | tf_op jit(solution)/shard_map/all_to_all | solution.py:142
  247.6 0.0 copy-done.1
  247.6 0.0 copy-start.3
  247.6 2.1 copy-done.3
  249.8 8.9 %experts.3 = bf16[512,2560]{1,0:T(8,128)(2,1)S(1)} custom-call(bf16[512,2560]{1,0:T(8,128)(2,1)S(1)} %bitcast.36, bf16[2560,768]{1,0:T(8,128)(2,1)S(1)} %bitcast.31, bf16[2560,768]{1,0:T(8,128)(2,1)S(1)} %bitcast.33, bf16[768,2560]{1,0:T(8,128)(2,1)} %bitcast.39), custom_call_target="tpu_custom_call" | custom-call | tf_op jit(solution)/shard_map/experts/pallas_call | solution.py:101
  258.6 68.3 %all_to_all.23 = bf16[64,8,2560]{2,1,0:T(8,128)(2,1)} all-to-all(bf16[64,8,2560]{2,1,0:T(8,128)(2,1)S(1)} %bitcast.37), channel_id=1, replica_groups=mesh['segment'=4,'expert'=32,'dp'=2] {'expert','dp'}, dimensions={0} | all-to-all | bytes 5242880 | tf_op jit(solution)/shard_map/all_to_all | solution.py:142
  326.9 0.0 copy-start.4
  326.9 3.3 combine.3
  330.2 0.0 copy-done.4
  330.2 1.9 maximum_bitcast_fusion
Async XLA Ops:
  5.2 75.3 %copy-start = (bf16[1,1,2560,768]{3,2,1,0:T(8,128)(2,1)S(1)}, bf16[1,1,2560,768]{3,2,1,0:T(8,128)(2,1)}, u32[]{:S(2)}) copy-start(bf16[1,1,2560,768]{3,2,1,0:T(8,128)(2,1)} %param.10) | copy-start | bytes 11796484
  80.5 2.1 copy-start.2
  163.0 11.0 %collective-permute-start = (bf16[64,2560]{1,0:T(8,128)(2,1)}, bf16[64,2560]{1,0:T(8,128)(2,1)S(1)}, u32[]{:S(2)}, u32[]{:S(2)}) collective-permute-start(bf16[64,2560]{1,0:T(8,128)(2,1)} %combine.2), channel_id=1, source_target_pairs={{0,64},{64,128},{128,192},{1,65},{65,129},{129,193},{2,66},{66,130... | collective-permute-start | bytes 983048 | tf_op jit(solution)/shard_map/ppermute | solution.py:157
  174.0 0.7 copy-start.5
  178.6 69.0 %copy-start.1 = (bf16[1,1,2560,768]{3,2,1,0:T(8,128)(2,1)S(1)}, bf16[1,1,2560,768]{3,2,1,0:T(8,128)(2,1)}, u32[]{:S(2)}) copy-start(bf16[1,1,2560,768]{3,2,1,0:T(8,128)(2,1)} %param.10) | copy-start | bytes 11796484
  247.6 2.1 copy-start.3
  326.9 3.3 copy-start.4

commit v2 on v1

v2 whole, which is shorter than its diff:
```python
import jax
import jax.numpy as jnp
from jax import lax
from jax.experimental import pallas as pl
from jax.experimental.pallas import tpu as pltpu
from jax.sharding import PartitionSpec as P

CAP = 8
LANES = 128
GROUP = ("expert", "dp")
Z, Y, C = 8, 4, 2
VMEM = pl.BlockSpec(memory_space=pltpu.VMEM)
SMEM = pl.BlockSpec(memory_space=pltpu.SMEM)


def dot(lhs, rhs, lhs_dim=1, rhs_dim=0):
    return lax.dot_general(
        lhs, rhs, (((lhs_dim,), (rhs_dim,)), ((), ())), preferred_element_type=jnp.float32
    )


def column_tiles(width, tile):
    return [slice(start, min(start + tile, width)) for start in range(0, width, tile)]


def iota(shape, dim):
    return lax.broadcasted_iota(jnp.int32, shape, dim)


def move(value, target):
    pairs = []
    for z in range(Z):
        for y in range(Y):
            for core in range(C):
                to_z, to_y, to_core = target(z, y, core)
                pairs.append(((z * Y + y) * C + core, ((to_z % Z) * Y + to_y % Y) * C + to_core))
    return lax.ppermute(value, GROUP, pairs)


def to_other_core(value):
    return move(value, lambda z, y, core: (z, y, 1 - core))


def along_y(value, steps):
    return value if steps == 0 else move(value, lambda z, y, core: (z, y + steps, core))


def outward(value):
    return move(value, lambda z, y, core: (z + 1 - 2 * core, y, core))


def homeward(value):
    return move(value, lambda z, y, core: (z - 1 + 2 * core, y, core))


def prepare_kernel(first_ref, arrived_ref, fresh_ref, gain_ref, router_ref, picks_ref,
                   current_ref, packed_ref):
    tokens, width = current_ref.shape
    experts = router_ref.shape[0]
    current = jnp.where(first_ref[0] == 1, fresh_ref[...], arrived_ref[...])
    current_ref[...] = current
    values = current.astype(jnp.float32)
    inv_scale = lax.rsqrt(jnp.mean(values * values, axis=1, keepdims=True) + 1e-06)
    normed = (values * inv_scale * gain_ref[...]).astype(jnp.bfloat16)
    packed_ref[:, :width] = normed
    logits = dot(normed, router_ref[...], 1, 1)
    expert_ids = iota((experts, tokens), 0)
    chosen_rows = jnp.zeros((experts, tokens), jnp.float32)
    for choice in range(picks_ref.shape[0]):
        chosen_rows += jnp.where(picks_ref[choice : choice + 1, :] == expert_ids, 1.0, 0.0)
    chosen_rows = chosen_rows.astype(jnp.bfloat16)
    row, column = iota((tokens, tokens), 0), iota((tokens, tokens), 1)
    chosen = dot(jnp.where(row == column, 1.0, 0.0).astype(jnp.bfloat16), chosen_rows, 1, 1)
    rank = dot(jnp.where(column < row, 1.0, 0.0).astype(jnp.bfloat16), chosen_rows, 1, 1)
    scores = chosen / (1.0 + jnp.exp(-logits))
    mixing = scores / jnp.sum(scores, axis=1, keepdims=True)
    slot = jnp.where(chosen > 0.0, rank, float(CAP))
    packed_ref[:, width:] = jnp.concatenate([slot, mixing], axis=1).astype(jnp.bfloat16)


def prepare(first, arrived, fresh, gain, router, picks):
    tokens, width = arrived.shape
    return pl.pallas_call(
        prepare_kernel,
        out_shape=(
            jax.ShapeDtypeStruct((tokens, width), jnp.bfloat16),
            jax.ShapeDtypeStruct((tokens, width + LANES), jnp.bfloat16),
        ),
        in_specs=[SMEM] + [VMEM] * 5,
        out_specs=(VMEM, VMEM),
        name="prepare",
    )(first, arrived, fresh, gain, router, picks)


def dispatch_kernel(block, count, ids_ref, *refs):
    packed_refs, row_refs, weights_ref = refs[:count], refs[count : count + Y], refs[count + Y]
    width = row_refs[0].shape[1]
    rows = row_refs[0].shape[0]
    notes = jnp.concatenate([ref[:, width:] for ref in packed_refs], axis=0)
    tokens = notes.shape[0]
    line, lane = iota((16, LANES), 0), iota((16, LANES), 1)
    select = jnp.zeros((16, LANES), jnp.float32)
    for step in range(Y):
        hit = (line == step) & (lane == ids_ref[step])
        hit |= (line == step + 8) & (lane == ids_ref[step] + LANES // 2)
        select = jnp.where(hit, 1.0, select)
    picked = dot(select.astype(jnp.bfloat16), notes, 1, 1)
    row, token = iota((rows, tokens), 0), iota((rows, tokens), 1)
    code = jnp.where(token // block == row // CAP, row % CAP, -1).astype(jnp.float32)
    picks = []
    for step in range(Y):
        here = jnp.broadcast_to(picked[step : step + 1, :], (rows, tokens)) == code
        mixing = jnp.broadcast_to(picked[step + 8 : step + 9, :], (rows, tokens))
        picks.append(jnp.where(here, 1.0, 0.0))
        weights_ref[step * rows : (step + 1) * rows, :] = jnp.where(here, mixing, 0.0).astype(jnp.bfloat16)
    pick = jnp.concatenate(picks, axis=0).astype(jnp.bfloat16)
    for cols in column_tiles(width, 512):
        values = jnp.concatenate([ref[:, cols] for ref in packed_refs], axis=0)
        result = dot(pick, values).astype(jnp.bfloat16)
        for step in range(Y):
            row_refs[step][:, cols] = result[step * rows : (step + 1) * rows]


def dispatch(ids, packed, block):
    width = packed[0].shape[1] - LANES
    tokens = sum(value.shape[0] for value in packed)
    rows = tokens // block * CAP
    result = pl.pallas_call(
        lambda *refs: dispatch_kernel(block, len(packed), *refs),
        out_shape=[jax.ShapeDtypeStruct((rows, width), jnp.bfloat16)] * Y
        + [jax.ShapeDtypeStruct((Y * rows, tokens), jnp.bfloat16)],
        in_specs=[SMEM] + [VMEM] * len(packed),
        out_specs=[VMEM] * (Y + 1),
        name="dispatch",
    )(ids, *packed)
    return result[:Y], result[Y]


def experts_kernel(count, *refs):
    row_refs, gate_ref, up_ref, down_ref = refs[:count], refs[count], refs[count + 1], refs[count + 2]
    out_refs, held_ref, total_ref = refs[count + 3 : 2 * count + 3], refs[2 * count + 3], refs[2 * count + 4]
    step, steps = pl.program_id(0), pl.num_programs(0)
    width = total_ref.shape[1]
    starts = [0]
    for ref in row_refs:
        starts.append(starts[-1] + ref.shape[0])

    @pl.when(step == 0)
    def _():
        for index, ref in enumerate(row_refs):
            held_ref[starts[index] : starts[index + 1], :] = ref[...]

    rows = held_ref[...]
    gate = dot(rows, gate_ref[...])
    up = dot(rows, up_ref[...])
    hidden = (gate / (1.0 + jnp.exp(-gate)) * up).astype(jnp.bfloat16)

    @pl.when(step == 0)
    def _():
        for cols in column_tiles(width, 512):
            total_ref[:, cols] = dot(hidden, down_ref[:, cols])

    @pl.when((step > 0) & (step < steps - 1))
    def _():
        for cols in column_tiles(width, 512):
            total_ref[:, cols] += dot(hidden, down_ref[:, cols])

    @pl.when(step == steps - 1)
    def _():
        for cols in column_tiles(width, 512):
            result = (total_ref[:, cols] + dot(hidden, down_ref[:, cols])).astype(jnp.bfloat16)
            for index, ref in enumerate(out_refs):
                ref[:, cols] = result[starts[index] : starts[index + 1]]


def run_experts(row_arrays, w_gate, w_up, w_down):
    width, hidden = w_gate.shape
    count = sum(value.shape[0] for value in row_arrays)
    tile = 256
    whole = [pl.BlockSpec(value.shape, lambda i: (0, 0)) for value in row_arrays]
    return pl.pallas_call(
        lambda *refs: experts_kernel(len(row_arrays), *refs),
        out_shape=[jax.ShapeDtypeStruct(value.shape, jnp.bfloat16) for value in row_arrays],
        grid_spec=pltpu.PrefetchScalarGridSpec(
            num_scalar_prefetch=0,
            grid=(hidden // tile,),
            in_specs=whole
            + [
                pl.BlockSpec((width, tile), lambda i: (0, i)),
                pl.BlockSpec((width, tile), lambda i: (0, i)),
                pl.BlockSpec((tile, width), lambda i: (i, 0)),
            ],
            out_specs=whole,
            scratch_shapes=[pltpu.VMEM((count, width), jnp.bfloat16), pltpu.VMEM((count, width), jnp.float32)],
        ),
        compiler_params=pltpu.CompilerParams(vmem_limit_bytes=40 << 20),
        name="experts",
    )(*row_arrays, w_gate, w_up, w_down)


def combine_kernel(weights_ref, *refs):
    landed_refs, out_refs = refs[:Y], refs[Y:]
    weights = jnp.transpose(weights_ref[...])
    for cols in column_tiles(landed_refs[0].shape[1], 512):
        landed = jnp.concatenate([ref[:, cols] for ref in landed_refs], axis=0)
        total = dot(weights, landed).astype(jnp.bfloat16)
        start = 0
        for ref in out_refs:
            ref[:, cols] = total[start : start + ref.shape[0]]
            start += ref.shape[0]


def combine(weights, landed, sizes):
    width = landed[0].shape[1]
    return pl.pallas_call(
        combine_kernel,
        out_shape=[jax.ShapeDtypeStruct((size, width), jnp.bfloat16) for size in sizes],
        in_specs=[VMEM] * (1 + Y),
        out_specs=[VMEM] * len(sizes),
        name="combine",
    )(weights, *landed)


def wide(value):
    return value.astype(jnp.float32)


def section(first, arrived, fresh, gain, router, picks, ids, w_gate, w_up, w_down):
    tokens = arrived.shape[0]
    current, packed = prepare(first, arrived, fresh, gain, router, picks)
    near = jnp.concatenate([packed, to_other_core(packed)], axis=0)
    one = outward(near)
    two = outward(one)
    three = outward(two)
    four = outward(three[:tokens])
    chunks = [
        [near, one, to_other_core(one)],
        [two, to_other_core(two)],
        [three, to_other_core(three)],
        [four, to_other_core(four)],
    ]
    rows, weights = [], []
    for chunk in chunks:
        sent, weight = dispatch(ids, chunk, tokens)
        rows.append([along_y(value, step) for step, value in enumerate(sent)])
        weights.append(weight)
    early = run_experts(rows[0] + rows[1], w_gate, w_up, w_down)
    late = run_experts(rows[2] + rows[3], w_gate, w_up, w_down)
    outputs = [early[:Y], early[Y:], late[:Y], late[Y:]]
    parts = []
    for chunk, weight, output in zip(chunks, weights, outputs):
        landed = [along_y(value, -step) for step, value in enumerate(output)]
        parts.append(combine(weight, landed, [value.shape[0] for value in chunk]))
    part = [wide(kept) + wide(to_other_core(sent)) for *_, kept, sent in parts]
    stream = homeward(part[3].astype(jnp.bfloat16))
    total = part[2] + jnp.pad(wide(stream), ((0, tokens), (0, 0)))
    stream = homeward(total.astype(jnp.bfloat16))
    stream = homeward((part[1] + wide(stream)).astype(jnp.bfloat16))
    stream = homeward((part[0] + wide(stream)).astype(jnp.bfloat16))
    held = wide(stream) + wide(parts[0][0])
    other = to_other_core(held[tokens:].astype(jnp.bfloat16))
    return (wide(current) + held[:tokens] + wide(other)).astype(jnp.bfloat16)


def shards(entering, fresh, w_gate, w_up, w_down, router, gain, routes):
    at_start = (lax.axis_index("segment") == 0).astype(jnp.int32).reshape(1)
    never = jnp.zeros((1,), jnp.int32)
    place, core = lax.axis_index("expert"), lax.axis_index("dp")
    z, y = place // Y, place % Y
    ids = (z * Y + (y + jnp.arange(Y, dtype=jnp.int32)) % Y) * C + core
    router_rows = jnp.transpose(router[0])
    picks = jnp.transpose(routes[0], (0, 2, 1))
    results = []
    count = lax.axis_size("segment")
    for step in range(routes.shape[1]):
        if step == 0:
            first, arrived, other = never, entering[0], entering[0]
        else:
            arrived = lax.ppermute(results[-1], "segment", [(i, i + 1) for i in range(count - 1)])
            first, other = at_start, fresh[step - 1]
        results.append(
            section(first, arrived, other, gain, router_rows, picks[step], ids, w_gate[0, 0], w_up[0, 0], w_down[0, 0])
        )
    return jnp.stack(results)[None]


def solution(mesh):
    tokens = P("segment", ("expert", "dp"), None)
    weights = P("segment", ("expert", "dp"), None, None)
    in_specs = (
        tokens, P(None, ("expert", "dp"), None), weights, weights, weights,
        P("segment", None, None), P("segment", None), P("segment", None, ("expert", "dp"), None),
    )
    out_specs = P("segment", None, ("expert", "dp"), None)
    return jax.shard_map(shards, mesh=mesh, in_specs=in_specs, out_specs=out_specs, check_vma=False)
```

time: 333 us -> 453 us (1.36); the launches traced: 332 us -> 444 us
  blocking collectives: 281 us -> 0 us
  waiting for transfers between devices: 9.75 us -> 220 us
  starting transfers between devices: 1.28 us -> 107 us
  Pallas kernels: 32 us -> 69.9 us
  local copies, waits for them, and re-layouts: 6.26 us -> 37.9 us
  other arithmetic: 1.87 us -> 8.85 us
    all_to_all x4 -> x0, blocking collectives: 281 us -> none  [exchange(): lax.all_to_all(parts, GROUP, split_axis=0, concat_axis=0, tiled=True)]
    ppermute x0 -> x84, waiting for transfers between devices: none -> 210 us  [move(): return lax.ppermute(value, GROUP, pairs)]
    ppermute x0 -> x84, starting transfers between devices: none -> 106 us  [move(): return lax.ppermute(value, GROUP, pairs)]
    pallas_call x4 -> x20, Pallas kernels: 24.3 us -> 64.9 us  [the longest x8 21.9 us: combine(): pl.pallas_call(combine_kernel, out_shape=[jax.ShapeDtypeStruct((size, wid...]
    unnamed x13 -> x147, local copies, waits for them, and re-layouts: 5.65 us -> 37.1 us
    convert_element_type x0 -> x9, other arithmetic: none -> 6.92 us  [the longest x2 4.25 us: section(): stream = homeward(total.astype(jnp.bfloat16))]
  transfers between devices with their start and end apart: 1 -> 85, of which waited for: 1 -> 47; matrix products, arithmetic and copies ran while one was open for 0% -> 2% of each run, Pallas kernels for 0% -> 15%
where the time goes in v2:
time: 453 us; the launch traced here: 444 us
  waiting for transfers between devices  220 us (49%)
  starting transfers between devices  107 us (24%)
  Pallas kernels  69.9 us (15%)
  local copies, waits for them, and re-layouts  37.9 us (8%)
  other arithmetic  8.85 us (2%)
    ppermute x84, waiting for transfers between devices, move(): return lax.ppermute(value, GROUP, pairs)  210 us
    ppermute x84, starting transfers between devices, move(): return lax.ppermute(value, GROUP, pairs)  106 us
    unnamed x147, local copies, waits for them, and re-layouts  37.1 us
    pallas_call x8, Pallas kernels, combine(): pl.pallas_call(combine_kernel, out_shape=[jax.ShapeDtypeStruct((size, wid...  21.9 us
    pallas_call x4, Pallas kernels, run_experts(): pl.pallas_call(lambda *refs: experts_kernel(len(row_arrays), *refs), out_...  21.6 us
    pallas_call x8, Pallas kernels, dispatch(): pl.pallas_call(lambda *refs: dispatch_kernel(block, len(packed), *refs),...  21.4 us
    ppermute x1, waiting for transfers between devices, shards(): lax.ppermute(results[-1], 'segment', [(i, i + 1) for i in range(count - 1)])  9.76 us
  transfers between devices with their start and end apart: 85, of which 47 were waited for; matrix products, arithmetic and copies ran while one was open for 2% of the time, Pallas kernels for 15%

profile of v2, /device:TPU:7, one launch (start us, length us, event | category | flops | bytes accessed | tf_op | source)
XLA Modules:
  0.0 444.3 jit_solution(709024493469435072)
XLA Ops:
  6.0 5.7 %collective-permute-start.1 = (bf16[128,2688]{1,0:T(8,128)(2,1)S(1)}, bf16[128,2688]{1,0:T(8,128)(2,1)S(1)}, u32[]{:S(2)}, u32[]{:S(2)}) collective-permute-start(bf16[128,2688]{1,0:T(8,128)(2,1)S(1)} %constant_dynamic-update-slice_fusion.refs_1_), channel_id=1, source_target_pairs={{0,8},{1,57},{2,10},{3,59},{4,12},{5,61},{6,14},{7,63},{8,16},{9,1... | collective-permute-start | bytes 2064392 | tf_op jit(solution)/shard_map/ppermute | solution.py:37
  11.6 7.9 %collective-permute-done.1.refs_2_ = bf16[128,2688]{1,0:T(8,128)(2,1)S(1)} collective-permute-done((bf16[128,2688]{1,0:T(8,128)(2,1)S(1)}, bf16[128,2688]{1,0:T(8,128)(2,1)S(1)}, u32[]{:S(2)}, u32[]{:S(2)}) %collective-permute-start.1) | collective-permute-done | bytes 688160 | tf_op jit(solution)/shard_map/ppermute | solution.py:37
  22.6 7.9 %collective-permute-done.6.refs_1_ = bf16[128,2688]{1,0:T(8,128)(2,1)S(1)} collective-permute-done((bf16[128,2688]{1,0:T(8,128)(2,1)S(1)}, bf16[128,2688]{1,0:T(8,128)(2,1)S(1)}, u32[]{:S(2)}, u32[]{:S(2)}) %collective-permute-start.6) | collective-permute-done | bytes 688160 | tf_op jit(solution)/shard_map/ppermute | solution.py:37
  33.6 7.9 %collective-permute-done.19.refs_1_ = bf16[128,2688]{1,0:T(8,128)(2,1)S(1)} collective-permute-done((bf16[128,2688]{1,0:T(8,128)(2,1)S(1)}, bf16[128,2688]{1,0:T(8,128)(2,1)S(1)}, u32[]{:S(2)}, u32[]{:S(2)}) %collective-permute-start.19) | collective-permute-done | bytes 688160 | tf_op jit(solution)/shard_map/ppermute | solution.py:37
  48.9 5.2 %collective-permute-start.25 = (bf16[64,2688]{1,0:T(8,128)(2,1)}, bf16[64,2688]{1,0:T(8,128)(2,1)}, u32[]{:S(2)}, u32[]{:S(2)}) collective-permute-start(bf16[64,2688]{1,0:T(8,128)(2,1)} %collective-permute-done.24.refs_1_), channel_id=1, source_target_pairs={{0,1},{1,0},{2,3},{3,2},{4,5},{5,4},{6,7},{7,6},{8,9},{9,8},{10,11... | collective-permute-start | bytes 1032200 | tf_op jit(solution)/shard_map/ppermute | solution.py:37
  69.2 6.9 %collective-permute-done.21.refs_1_ = bf16[32,2560]{1,0:T(8,128)(2,1)S(1)} collective-permute-done((bf16[32,2560]{1,0:T(8,128)(2,1)}, bf16[32,2560]{1,0:T(8,128)(2,1)S(1)}, u32[]{:S(2)}, u32[]{:S(2)}) %collective-permute-start.21) | collective-permute-done | bytes 163872 | tf_op jit(solution)/shard_map/ppermute | solution.py:37
  83.4 4.1 experts.5
  112.7 10.4 %collective-permute-done.30.refs_2_ = bf16[32,2560]{1,0:T(8,128)(2,1)S(1)} collective-permute-done((bf16[32,2560]{1,0:T(8,128)(2,1)S(1)}, bf16[32,2560]{1,0:T(8,128)(2,1)S(1)}, u32[]{:S(2)}, u32[]{:S(2)}) %collective-permute-start.30) | collective-permute-done | bytes 163872 | tf_op jit(solution)/shard_map/ppermute | solution.py:37
  123.2 4.7 %collective-permute-done.31.refs_3_ = bf16[32,2560]{1,0:T(8,128)(2,1)S(1)} collective-permute-done((bf16[32,2560]{1,0:T(8,128)(2,1)S(1)}, bf16[32,2560]{1,0:T(8,128)(2,1)S(1)}, u32[]{:S(2)}, u32[]{:S(2)}) %collective-permute-start.31) | collective-permute-done | bytes 163872 | tf_op jit(solution)/shard_map/ppermute | solution.py:37
  145.5 6.8 %experts.4 = (bf16[48,2560]{1,0:T(8,128)(2,1)S(1)}, bf16[48,2560]{1,0:T(8,128)(2,1)S(1)}, bf16[48,2560]{1,0:T(8,128)(2,1)S(1)}, bf16[48,2560]{1,0:T(8,128)(2,1)S...) custom-call(bf16[48,2560]{1,0:T(8,128)(2,1)S(1)} %copy-done.11, ...), custom_call_target="tpu_custom_call" | custom-call | tf_op jit(solution)/shard_map/experts/pallas_call | solution.py:181
  157.6 6.2 %collective-permute-done.15.refs_1_ = bf16[32,2560]{1,0:T(8,128)(2,1)S(1)} collective-permute-done((bf16[32,2560]{1,0:T(8,128)(2,1)S(1)}, bf16[32,2560]{1,0:T(8,128)(2,1)S(1)}, u32[]{:S(2)}, u32[]{:S(2)}) %collective-permute-start.15) | collective-permute-done | bytes 163872 | tf_op jit(solution)/shard_map/ppermute | solution.py:37
  175.3 6.1 %collective-permute-done.11.refs_1_ = bf16[48,2560]{1,0:T(8,128)(2,1)S(1)} collective-permute-done((bf16[48,2560]{1,0:T(8,128)(2,1)S(1)}, bf16[48,2560]{1,0:T(8,128)(2,1)S(1)}, u32[]{:S(2)}, u32[]{:S(2)}) %collective-permute-start.11) | collective-permute-done | bytes 245792 | tf_op jit(solution)/shard_map/ppermute | solution.py:37
  183.3 5.9 %collective-permute-done.13.refs_3_ = bf16[48,2560]{1,0:T(8,128)(2,1)S(1)} collective-permute-done((bf16[48,2560]{1,0:T(8,128)(2,1)S(1)}, bf16[48,2560]{1,0:T(8,128)(2,1)S(1)}, u32[]{:S(2)}, u32[]{:S(2)}) %collective-permute-start.13) | collective-permute-done | bytes 245792 | tf_op jit(solution)/shard_map/ppermute | solution.py:37
  195.5 9.2 %collective-permute-done.39 = bf16[128,2560]{1,0:T(8,128)(2,1)S(1)} collective-permute-done((bf16[128,2560]{1,0:T(8,128)(2,1)S(1)}, bf16[128,2560]{1,0:T(8,128)(2,1)S(1)}, u32[]{:S(2)}, u32[]{:S(2)}) %collective-permute-start.39) | collective-permute-done | bytes 655392 | tf_op jit(solution)/shard_map/ppermute | solution.py:37
  205.1 10.6 %collective-permute-done.40 = bf16[128,2560]{1,0:T(8,128)(2,1)S(1)} collective-permute-done((bf16[128,2560]{1,0:T(8,128)(2,1)S(1)}, bf16[128,2560]{1,0:T(8,128)(2,1)S(1)}, u32[]{:S(2)}, u32[]{:S(2)}) %collective-permute-start.40) | collective-permute-done | bytes 655392 | tf_op jit(solution)/shard_map/ppermute | solution.py:37
  219.0 9.8 %collective-permute-done.42.arrived_ref = bf16[64,2560]{1,0:T(8,128)(2,1)S(1)} collective-permute-done((bf16[64,2560]{1,0:T(8,128)(2,1)S(1)}, bf16[64,2560]{1,0:T(8,128)(2,1)S(1)}, u32[]{:S(2)}, u32[]{:S(2)}) %collective-permute-start.42) | collective-permute-done | bytes 327712 | tf_op jit(solution)/shard_map/ppermute | solution.py:279
  236.8 8.0 %collective-permute-done.44.refs_2_ = bf16[128,2688]{1,0:T(8,128)(2,1)} collective-permute-done((bf16[128,2688]{1,0:T(8,128)(2,1)S(1)}, bf16[128,2688]{1,0:T(8,128)(2,1)}, u32[]{:S(2)}, u32[]{:S(2)}) %collective-permute-start.44) | collective-permute-done | bytes 688160 | tf_op jit(solution)/shard_map/ppermute | solution.py:37
  247.9 8.2 %collective-permute-done.49.refs_1_ = bf16[128,2688]{1,0:T(8,128)(2,1)S(1)} collective-permute-done((bf16[128,2688]{1,0:T(8,128)(2,1)}, bf16[128,2688]{1,0:T(8,128)(2,1)S(1)}, u32[]{:S(2)}, u32[]{:S(2)}) %collective-permute-start.49) | collective-permute-done | bytes 688160 | tf_op jit(solution)/shard_map/ppermute | solution.py:37
  259.1 7.9 %collective-permute-done.62.refs_1_ = bf16[128,2688]{1,0:T(8,128)(2,1)S(1)} collective-permute-done((bf16[128,2688]{1,0:T(8,128)(2,1)S(1)}, bf16[128,2688]{1,0:T(8,128)(2,1)S(1)}, u32[]{:S(2)}, u32[]{:S(2)}) %collective-permute-start.62) | collective-permute-done | bytes 688160 | tf_op jit(solution)/shard_map/ppermute | solution.py:37
  274.4 5.9 %collective-permute-start.68 = (bf16[64,2688]{1,0:T(8,128)(2,1)S(1)}, bf16[64,2688]{1,0:T(8,128)(2,1)}, u32[]{:S(2)}, u32[]{:S(2)}) collective-permute-start(bf16[64,2688]{1,0:T(8,128)(2,1)S(1)} %collective-permute-done.67.refs_1_), channel_id=1, source_target_pairs={{0,1},{1,0},{2,3},{3,2},{4,5},{5,4},{6,7},{7,6},{8,9},{9,8},{10,11... | collective-permute-start | bytes 1032200 | tf_op jit(solution)/shard_map/ppermute | solution.py:37
  294.7 7.0 %collective-permute-done.64.refs_1_ = bf16[32,2560]{1,0:T(8,128)(2,1)S(1)} collective-permute-done((bf16[32,2560]{1,0:T(8,128)(2,1)}, bf16[32,2560]{1,0:T(8,128)(2,1)S(1)}, u32[]{:S(2)}, u32[]{:S(2)}) %collective-permute-start.64) | collective-permute-done | bytes 163872 | tf_op jit(solution)/shard_map/ppermute | solution.py:37
  309.2 4.1 experts.7
  319.7 4.8 %collective-permute-start.72 = (bf16[32,2560]{1,0:T(8,128)(2,1)S(1)}, bf16[32,2560]{1,0:T(8,128)(2,1)S(1)}, u32[]{:S(2)}, u32[]{:S(2)}) collective-permute-start(bf16[32,2560]{1,0:T(8,128)(2,1)S(1)} %get-tuple-element.180), channel_id=1, source_target_pairs={{0,6},{1,7},{2,0},{3,1},{4,2},{5,3},{6,4},{7,5},{8,14},{9,15},{10,... | collective-permute-start | bytes 491528 | tf_op jit(solution)/shard_map/ppermute | solution.py:37
  338.2 10.6 %collective-permute-done.73.refs_2_ = bf16[32,2560]{1,0:T(8,128)(2,1)S(1)} collective-permute-done((bf16[32,2560]{1,0:T(8,128)(2,1)S(1)}, bf16[32,2560]{1,0:T(8,128)(2,1)S(1)}, u32[]{:S(2)}, u32[]{:S(2)}) %collective-permute-start.73) | collective-permute-done | bytes 163872 | tf_op jit(solution)/shard_map/ppermute | solution.py:37
  348.8 4.7 %collective-permute-done.74.refs_3_ = bf16[32,2560]{1,0:T(8,128)(2,1)S(1)} collective-permute-done((bf16[32,2560]{1,0:T(8,128)(2,1)S(1)}, bf16[32,2560]{1,0:T(8,128)(2,1)S(1)}, u32[]{:S(2)}, u32[]{:S(2)}) %collective-permute-start.74) | collective-permute-done | bytes 163872 | tf_op jit(solution)/shard_map/ppermute | solution.py:37
  371.1 6.8 %experts.6 = (bf16[48,2560]{1,0:T(8,128)(2,1)S(1)}, bf16[48,2560]{1,0:T(8,128)(2,1)S(1)}, bf16[48,2560]{1,0:T(8,128)(2,1)S(1)}, bf16[48,2560]{1,0:T(8,128)(2,1)S...) custom-call(bf16[48,2560]{1,0:T(8,128)(2,1)S(1)} %copy-done.10, ...), custom_call_target="tpu_custom_call" | custom-call | tf_op jit(solution)/shard_map/experts/pallas_call | solution.py:181
  383.1 6.2 %collective-permute-done.58.refs_1_ = bf16[32,2560]{1,0:T(8,128)(2,1)S(1)} collective-permute-done((bf16[32,2560]{1,0:T(8,128)(2,1)S(1)}, bf16[32,2560]{1,0:T(8,128)(2,1)S(1)}, u32[]{:S(2)}, u32[]{:S(2)}) %collective-permute-start.58) | collective-permute-done | bytes 163872 | tf_op jit(solution)/shard_map/ppermute | solution.py:37
  389.3 3.7 collective-permute-done.60.refs_3_
  400.9 6.1 %collective-permute-done.54.refs_1_ = bf16[48,2560]{1,0:T(8,128)(2,1)S(1)} collective-permute-done((bf16[48,2560]{1,0:T(8,128)(2,1)S(1)}, bf16[48,2560]{1,0:T(8,128)(2,1)S(1)}, u32[]{:S(2)}, u32[]{:S(2)}) %collective-permute-start.54) | collective-permute-done | bytes 245792 | tf_op jit(solution)/shard_map/ppermute | solution.py:37
  408.9 5.9 %collective-permute-done.56.refs_3_ = bf16[48,2560]{1,0:T(8,128)(2,1)S(1)} collective-permute-done((bf16[48,2560]{1,0:T(8,128)(2,1)S(1)}, bf16[48,2560]{1,0:T(8,128)(2,1)S(1)}, u32[]{:S(2)}, u32[]{:S(2)}) %collective-permute-start.56) | collective-permute-done | bytes 245792 | tf_op jit(solution)/shard_map/ppermute | solution.py:37
  421.1 9.1 %collective-permute-done.82 = bf16[128,2560]{1,0:T(8,128)(2,1)S(1)} collective-permute-done((bf16[128,2560]{1,0:T(8,128)(2,1)S(1)}, bf16[128,2560]{1,0:T(8,128)(2,1)S(1)}, u32[]{:S(2)}, u32[]{:S(2)}) %collective-permute-start.82) | collective-permute-done | bytes 655392 | tf_op jit(solution)/shard_map/ppermute | solution.py:37
  430.5 10.6 %collective-permute-done.83 = bf16[128,2560]{1,0:T(8,128)(2,1)S(1)} collective-permute-done((bf16[128,2560]{1,0:T(8,128)(2,1)S(1)}, bf16[128,2560]{1,0:T(8,128)(2,1)S(1)}, u32[]{:S(2)}, u32[]{:S(2)}) %collective-permute-start.83) | collective-permute-done | bytes 655392 | tf_op jit(solution)/shard_map/ppermute | solution.py:37
  (328 shorter events, 218.9 us)
Async XLA Ops:
  6.0 13.5 %collective-permute-start.1 = (bf16[128,2688]{1,0:T(8,128)(2,1)S(1)}, bf16[128,2688]{1,0:T(8,128)(2,1)S(1)}, u32[]{:S(2)}, u32[]{:S(2)}) collective-permute-start(bf16[128,2688]{1,0:T(8,128)(2,1)S(1)} %constant_dynamic-update-slice_fusion.refs_1_), channel_id=1, source_target_pairs={{0,8},{1,57},{2,10},{3,59},{4,12},{5,61},{6,14},{7,63},{8,16},{9,1... | collective-permute-start | bytes 2064392 | tf_op jit(solution)/shard_map/ppermute | solution.py:37
  44.7 17.6 %collective-permute-start.20 = (bf16[128,2688]{1,0:T(8,128)(2,1)S(1)}, bf16[128,2688]{1,0:T(8,128)(2,1)}, u32[]{:S(2)}, u32[]{:S(2)}) collective-permute-start(bf16[128,2688]{1,0:T(8,128)(2,1)S(1)} %collective-permute-done.19.refs_1_), channel_id=1, source_target_pairs={{0,1},{1,0},{2,3},{3,2},{4,5},{5,4},{6,7},{7,6},{8,9},{9,8},{10,11... | collective-permute-start | bytes 2064392 | tf_op jit(solution)/shard_map/ppermute | solution.py:37
  54.2 49.1 %collective-permute-start.2 = (bf16[128,2688]{1,0:T(8,128)(2,1)S(1)}, bf16[128,2688]{1,0:T(8,128)(2,1)}, u32[]{:S(2)}, u32[]{:S(2)}) collective-permute-start(bf16[128,2688]{1,0:T(8,128)(2,1)S(1)} %collective-permute-done.1.refs_2_), channel_id=1, source_target_pairs={{0,1},{1,0},{2,3},{3,2},{4,5},{5,4},{6,7},{7,6},{8,9},{9,8},{10,11... | collective-permute-start | bytes 2064392 | tf_op jit(solution)/shard_map/ppermute | solution.py:37
  54.2 53.8 %collective-permute-start.7 = (bf16[128,2688]{1,0:T(8,128)(2,1)S(1)}, bf16[128,2688]{1,0:T(8,128)(2,1)}, u32[]{:S(2)}, u32[]{:S(2)}) collective-permute-start(bf16[128,2688]{1,0:T(8,128)(2,1)S(1)} %collective-permute-done.6.refs_1_), channel_id=1, source_target_pairs={{0,1},{1,0},{2,3},{3,2},{4,5},{5,4},{6,7},{7,6},{8,9},{9,8},{10,11... | collective-permute-start | bytes 2064392 | tf_op jit(solution)/shard_map/ppermute | solution.py:37
  94.1 15.5 %collective-permute-start.29 = (bf16[32,2560]{1,0:T(8,128)(2,1)S(1)}, bf16[32,2560]{1,0:T(8,128)(2,1)S(1)}, u32[]{:S(2)}, u32[]{:S(2)}) collective-permute-start(bf16[32,2560]{1,0:T(8,128)(2,1)S(1)} %get-tuple-element.133), channel_id=1, source_target_pairs={{0,6},{1,7},{2,0},{3,1},{4,2},{5,3},{6,4},{7,5},{8,14},{9,15},{10,... | collective-permute-start | bytes 491528 | tf_op jit(solution)/shard_map/ppermute | solution.py:37
  100.5 33.3 %collective-permute-start.36 = (bf16[64,2560]{1,0:T(8,128)(2,1)}, bf16[64,2560]{1,0:T(8,128)(2,1)S(1)}, u32[]{:S(2)}, u32[]{:S(2)}) collective-permute-start(bf16[64,2560]{1,0:T(8,128)(2,1)} %get-tuple-element.144), channel_id=1, source_target_pairs={{0,1},{1,0},{2,3},{3,2},{4,5},{5,4},{6,7},{7,6},{8,9},{9,8},{10,11... | collective-permute-start | bytes 983048 | tf_op jit(solution)/shard_map/ppermute | solution.py:37
  106.5 24.7 %collective-permute-start.3 = (bf16[48,2560]{1,0:T(8,128)(2,1)}, bf16[48,2560]{1,0:T(8,128)(2,1)S(1)}, u32[]{:S(2)}, u32[]{:S(2)}) collective-permute-start(bf16[48,2560]{1,0:T(8,128)(2,1)} %get-tuple-element.103), channel_id=1, source_target_pairs={{0,2},{1,3},{2,4},{3,5},{4,6},{5,7},{6,0},{7,1},{8,10},{9,11},{10,... | collective-permute-start | bytes 737288 | tf_op jit(solution)/shard_map/ppermute | solution.py:37
  106.5 24.7 %collective-permute-start.4 = (bf16[48,2560]{1,0:T(8,128)(2,1)}, bf16[48,2560]{1,0:T(8,128)(2,1)S(1)}, u32[]{:S(2)}, u32[]{:S(2)}) collective-permute-start(bf16[48,2560]{1,0:T(8,128)(2,1)} %get-tuple-element.104), channel_id=1, source_target_pairs={{0,4},{1,5},{2,6},{3,7},{4,0},{5,1},{6,2},{7,3},{8,12},{9,13},{10,... | collective-permute-start | bytes 737288 | tf_op jit(solution)/shard_map/ppermute | solution.py:37
  108.0 15.1 %collective-permute-start.30 = (bf16[32,2560]{1,0:T(8,128)(2,1)S(1)}, bf16[32,2560]{1,0:T(8,128)(2,1)S(1)}, u32[]{:S(2)}, u32[]{:S(2)}) collective-permute-start(bf16[32,2560]{1,0:T(8,128)(2,1)S(1)} %get-tuple-element.134), channel_id=1, source_target_pairs={{0,4},{1,5},{2,6},{3,7},{4,0},{5,1},{6,2},{7,3},{8,12},{9,13},{10,... | collective-permute-start | bytes 491528 | tf_op jit(solution)/shard_map/ppermute | solution.py:37
  109.6 18.2 %collective-permute-start.31 = (bf16[32,2560]{1,0:T(8,128)(2,1)S(1)}, bf16[32,2560]{1,0:T(8,128)(2,1)S(1)}, u32[]{:S(2)}, u32[]{:S(2)}) collective-permute-start(bf16[32,2560]{1,0:T(8,128)(2,1)S(1)} %get-tuple-element.135), channel_id=1, source_target_pairs={{0,2},{1,3},{2,4},{3,5},{4,6},{5,7},{6,0},{7,1},{8,10},{9,11},{10,... | collective-permute-start | bytes 491528 | tf_op jit(solution)/shard_map/ppermute | solution.py:37
  123.2 12.8 %collective-permute-start.5 = (bf16[48,2560]{1,0:T(8,128)(2,1)}, bf16[48,2560]{1,0:T(8,128)(2,1)S(1)}, u32[]{:S(2)}, u32[]{:S(2)}) collective-permute-start(bf16[48,2560]{1,0:T(8,128)(2,1)} %get-tuple-element.105), channel_id=1, source_target_pairs={{0,6},{1,7},{2,0},{3,1},{4,2},{5,3},{6,4},{7,5},{8,14},{9,15},{10,... | collective-permute-start | bytes 737288 | tf_op jit(solution)/shard_map/ppermute | solution.py:37
  133.8 38.0 %collective-permute-start.32 = (bf16[128,2560]{1,0:T(8,128)(2,1)}, bf16[128,2560]{1,0:T(8,128)(2,1)S(1)}, u32[]{:S(2)}, u32[]{:S(2)}) collective-permute-start(bf16[128,2560]{1,0:T(8,128)(2,1)} %get-tuple-element.137), channel_id=1, source_target_pairs={{0,1},{1,0},{2,3},{3,2},{4,5},{5,4},{6,7},{7,6},{8,9},{9,8},{10,11... | collective-permute-start | bytes 1966088 | tf_op jit(solution)/shard_map/ppermute | solution.py:37
  135.9 35.8 %collective-permute-start.37 = (bf16[64,2560]{1,0:T(8,128)(2,1)}, bf16[64,2560]{1,0:T(8,128)(2,1)}, u32[]{:S(2)}, u32[]{:S(2)}) collective-permute-start(bf16[64,2560]{1,0:T(8,128)(2,1)} %add_convert_fusion.7), channel_id=1, source_target_pairs={{0,56},{1,9},{2,58},{3,11},{4,60},{5,13},{6,62},{7,15},{8,0},{9,17... | collective-permute-start | bytes 983048 | tf_op jit(solution)/shard_map/ppermute | solution.py:37
  170.9 22.6 %collective-permute-start.18 = (bf16[128,2560]{1,0:T(8,128)(2,1)}, bf16[128,2560]{1,0:T(8,128)(2,1)S(1)}, u32[]{:S(2)}, u32[]{:S(2)}) collective-permute-start(bf16[128,2560]{1,0:T(8,128)(2,1)} %get-tuple-element.122), channel_id=1, source_target_pairs={{0,1},{1,0},{2,3},{3,2},{4,5},{5,4},{6,7},{7,6},{8,9},{9,8},{10,11... | collective-permute-start | bytes 1966088 | tf_op jit(solution)/shard_map/ppermute | solution.py:37
  173.8 19.7 %collective-permute-start.38 = (bf16[128,2560]{1,0:T(8,128)(2,1)}, bf16[128,2560]{1,0:T(8,128)(2,1)S(1)}, u32[]{:S(2)}, u32[]{:S(2)}) collective-permute-start(bf16[128,2560]{1,0:T(8,128)(2,1)} %add_convert_fusion.5), channel_id=1, source_target_pairs={{0,56},{1,9},{2,58},{3,11},{4,60},{5,13},{6,62},{7,15},{8,0},{9,17... | collective-permute-start | bytes 1966088 | tf_op jit(solution)/shard_map/ppermute | solution.py:37
  174.5 14.7 %collective-permute-start.13 = (bf16[48,2560]{1,0:T(8,128)(2,1)S(1)}, bf16[48,2560]{1,0:T(8,128)(2,1)S(1)}, u32[]{:S(2)}, u32[]{:S(2)}) collective-permute-start(bf16[48,2560]{1,0:T(8,128)(2,1)S(1)} %get-tuple-element.113), channel_id=1, source_target_pairs={{0,2},{1,3},{2,4},{3,5},{4,6},{5,7},{6,0},{7,1},{8,10},{9,11},{10,... | collective-permute-start | bytes 737288 | tf_op jit(solution)/shard_map/ppermute | solution.py:37
  244.8 11.3 %collective-permute-start.49 = (bf16[128,2688]{1,0:T(8,128)(2,1)}, bf16[128,2688]{1,0:T(8,128)(2,1)S(1)}, u32[]{:S(2)}, u32[]{:S(2)}) collective-permute-start(bf16[128,2688]{1,0:T(8,128)(2,1)} %collective-permute-done.44.refs_2_), channel_id=1, source_target_pairs={{0,8},{1,57},{2,10},{3,59},{4,12},{5,61},{6,14},{7,63},{8,16},{9,1... | collective-permute-start | bytes 2064392 | tf_op jit(solution)/shard_map/ppermute | solution.py:37
  270.2 15.7 %collective-permute-start.63 = (bf16[128,2688]{1,0:T(8,128)(2,1)S(1)}, bf16[128,2688]{1,0:T(8,128)(2,1)}, u32[]{:S(2)}, u32[]{:S(2)}) collective-permute-start(bf16[128,2688]{1,0:T(8,128)(2,1)S(1)} %collective-permute-done.62.refs_1_), channel_id=1, source_target_pairs={{0,1},{1,0},{2,3},{3,2},{4,5},{5,4},{6,7},{7,6},{8,9},{9,8},{10,11... | collective-permute-start | bytes 2064392 | tf_op jit(solution)/shard_map/ppermute | solution.py:37
  280.3 48.6 %collective-permute-start.45 = (bf16[128,2688]{1,0:T(8,128)(2,1)}, bf16[128,2688]{1,0:T(8,128)(2,1)}, u32[]{:S(2)}, u32[]{:S(2)}) collective-permute-start(bf16[128,2688]{1,0:T(8,128)(2,1)} %collective-permute-done.44.refs_2_), channel_id=1, source_target_pairs={{0,1},{1,0},{2,3},{3,2},{4,5},{5,4},{6,7},{7,6},{8,9},{9,8},{10,11... | collective-permute-start | bytes 2064392 | tf_op jit(solution)/shard_map/ppermute | solution.py:37
  280.3 53.3 %collective-permute-start.50 = (bf16[128,2688]{1,0:T(8,128)(2,1)S(1)}, bf16[128,2688]{1,0:T(8,128)(2,1)}, u32[]{:S(2)}, u32[]{:S(2)}) collective-permute-start(bf16[128,2688]{1,0:T(8,128)(2,1)S(1)} %collective-permute-done.49.refs_1_), channel_id=1, source_target_pairs={{0,1},{1,0},{2,3},{3,2},{4,5},{5,4},{6,7},{7,6},{8,9},{9,8},{10,11... | collective-permute-start | bytes 2064392 | tf_op jit(solution)/shard_map/ppermute | solution.py:37
  319.7 15.5 %collective-permute-start.72 = (bf16[32,2560]{1,0:T(8,128)(2,1)S(1)}, bf16[32,2560]{1,0:T(8,128)(2,1)S(1)}, u32[]{:S(2)}, u32[]{:S(2)}) collective-permute-start(bf16[32,2560]{1,0:T(8,128)(2,1)S(1)} %get-tuple-element.180), channel_id=1, source_target_pairs={{0,6},{1,7},{2,0},{3,1},{4,2},{5,3},{6,4},{7,5},{8,14},{9,15},{10,... | collective-permute-start | bytes 491528 | tf_op jit(solution)/shard_map/ppermute | solution.py:37
  327.4 31.7 %collective-permute-start.79 = (bf16[64,2560]{1,0:T(8,128)(2,1)}, bf16[64,2560]{1,0:T(8,128)(2,1)S(1)}, u32[]{:S(2)}, u32[]{:S(2)}) collective-permute-start(bf16[64,2560]{1,0:T(8,128)(2,1)} %get-tuple-element.191), channel_id=1, source_target_pairs={{0,1},{1,0},{2,3},{3,2},{4,5},{5,4},{6,7},{7,6},{8,9},{9,8},{10,11... | collective-permute-start | bytes 983048 | tf_op jit(solution)/shard_map/ppermute | solution.py:37
  332.1 24.7 %collective-permute-start.46 = (bf16[48,2560]{1,0:T(8,128)(2,1)}, bf16[48,2560]{1,0:T(8,128)(2,1)S(1)}, u32[]{:S(2)}, u32[]{:S(2)}) collective-permute-start(bf16[48,2560]{1,0:T(8,128)(2,1)} %get-tuple-element.150), channel_id=1, source_target_pairs={{0,2},{1,3},{2,4},{3,5},{4,6},{5,7},{6,0},{7,1},{8,10},{9,11},{10,... | collective-permute-start | bytes 737288 | tf_op jit(solution)/shard_map/ppermute | solution.py:37
  332.2 24.7 %collective-permute-start.47 = (bf16[48,2560]{1,0:T(8,128)(2,1)}, bf16[48,2560]{1,0:T(8,128)(2,1)S(1)}, u32[]{:S(2)}, u32[]{:S(2)}) collective-permute-start(bf16[48,2560]{1,0:T(8,128)(2,1)} %get-tuple-element.151), channel_id=1, source_target_pairs={{0,4},{1,5},{2,6},{3,7},{4,0},{5,1},{6,2},{7,3},{8,12},{9,13},{10,... | collective-permute-start | bytes 737288 | tf_op jit(solution)/shard_map/ppermute | solution.py:37
  333.6 15.1 %collective-permute-start.73 = (bf16[32,2560]{1,0:T(8,128)(2,1)S(1)}, bf16[32,2560]{1,0:T(8,128)(2,1)S(1)}, u32[]{:S(2)}, u32[]{:S(2)}) collective-permute-start(bf16[32,2560]{1,0:T(8,128)(2,1)S(1)} %get-tuple-element.181), channel_id=1, source_target_pairs={{0,4},{1,5},{2,6},{3,7},{4,0},{5,1},{6,2},{7,3},{8,12},{9,13},{10,... | collective-permute-start | bytes 491528 | tf_op jit(solution)/shard_map/ppermute | solution.py:37
  335.2 18.2 %collective-permute-start.74 = (bf16[32,2560]{1,0:T(8,128)(2,1)S(1)}, bf16[32,2560]{1,0:T(8,128)(2,1)S(1)}, u32[]{:S(2)}, u32[]{:S(2)}) collective-permute-start(bf16[32,2560]{1,0:T(8,128)(2,1)S(1)} %get-tuple-element.182), channel_id=1, source_target_pairs={{0,2},{1,3},{2,4},{3,5},{4,6},{5,7},{6,0},{7,1},{8,10},{9,11},{10,... | collective-permute-start | bytes 491528 | tf_op jit(solution)/shard_map/ppermute | solution.py:37
  348.7 12.5 %collective-permute-start.48 = (bf16[48,2560]{1,0:T(8,128)(2,1)S(1)}, bf16[48,2560]{1,0:T(8,128)(2,1)S(1)}, u32[]{:S(2)}, u32[]{:S(2)}) collective-permute-start(bf16[48,2560]{1,0:T(8,128)(2,1)S(1)} %copy-done.71), channel_id=1, source_target_pairs={{0,6},{1,7},{2,0},{3,1},{4,2},{5,3},{6,4},{7,5},{8,14},{9,15},{10,... | collective-permute-start | bytes 737288 | tf_op jit(solution)/shard_map/ppermute | solution.py:37
  359.1 38.1 %collective-permute-start.75 = (bf16[128,2560]{1,0:T(8,128)(2,1)}, bf16[128,2560]{1,0:T(8,128)(2,1)}, u32[]{:S(2)}, u32[]{:S(2)}) collective-permute-start(bf16[128,2560]{1,0:T(8,128)(2,1)} %get-tuple-element.184), channel_id=1, source_target_pairs={{0,1},{1,0},{2,3},{3,2},{4,5},{5,4},{6,7},{7,6},{8,9},{9,8},{10,11... | collective-permute-start | bytes 1966088 | tf_op jit(solution)/shard_map/ppermute | solution.py:37
  361.3 36.0 %collective-permute-start.80 = (bf16[64,2560]{1,0:T(8,128)(2,1)}, bf16[64,2560]{1,0:T(8,128)(2,1)S(1)}, u32[]{:S(2)}, u32[]{:S(2)}) collective-permute-start(bf16[64,2560]{1,0:T(8,128)(2,1)} %add_convert_fusion.6), channel_id=1, source_target_pairs={{0,56},{1,9},{2,58},{3,11},{4,60},{5,13},{6,62},{7,15},{8,0},{9,17... | collective-permute-start | bytes 983048 | tf_op jit(solution)/shard_map/ppermute | solution.py:37
  396.5 22.7 %collective-permute-start.61 = (bf16[128,2560]{1,0:T(8,128)(2,1)}, bf16[128,2560]{1,0:T(8,128)(2,1)S(1)}, u32[]{:S(2)}, u32[]{:S(2)}) collective-permute-start(bf16[128,2560]{1,0:T(8,128)(2,1)} %get-tuple-element.169), channel_id=1, source_target_pairs={{0,1},{1,0},{2,3},{3,2},{4,5},{5,4},{6,7},{7,6},{8,9},{9,8},{10,11... | collective-permute-start | bytes 1966088 | tf_op jit(solution)/shard_map/ppermute | solution.py:37
  399.5 19.7 %collective-permute-start.81 = (bf16[128,2560]{1,0:T(8,128)(2,1)}, bf16[128,2560]{1,0:T(8,128)(2,1)S(1)}, u32[]{:S(2)}, u32[]{:S(2)}) collective-permute-start(bf16[128,2560]{1,0:T(8,128)(2,1)} %add_convert_fusion.2), channel_id=1, source_target_pairs={{0,56},{1,9},{2,58},{3,11},{4,60},{5,13},{6,62},{7,15},{8,0},{9,17... | collective-permute-start | bytes 1966088 | tf_op jit(solution)/shard_map/ppermute | solution.py:37
  400.1 14.7 %collective-permute-start.56 = (bf16[48,2560]{1,0:T(8,128)(2,1)S(1)}, bf16[48,2560]{1,0:T(8,128)(2,1)S(1)}, u32[]{:S(2)}, u32[]{:S(2)}) collective-permute-start(bf16[48,2560]{1,0:T(8,128)(2,1)S(1)} %get-tuple-element.160), channel_id=1, source_target_pairs={{0,2},{1,3},{2,4},{3,5},{4,6},{5,7},{6,0},{7,1},{8,10},{9,11},{10,... | collective-permute-start | bytes 737288 | tf_op jit(solution)/shard_map/ppermute | solution.py:37
  (125 other events, 1263.5 us)

commit v3 on v1

v3 whole, which is shorter than its diff:
```python
import jax
import jax.numpy as jnp
from jax import lax
from jax.experimental import pallas as pl
from jax.experimental.pallas import tpu as pltpu
from jax.sharding import PartitionSpec as P

CAP = 8
GROUP = ("expert", "dp")


def dot(lhs, rhs, lhs_dim=1, rhs_dim=0):
    return lax.dot_general(
        lhs, rhs, (((lhs_dim,), (rhs_dim,)), ((), ())), preferred_element_type=jnp.float32
    )


def column_tiles(width, tile):
    return [slice(start, min(start + tile, width)) for start in range(0, width, tile)]


def prepare_kernel(step, first_ref, arrived_ref, fresh_ref, gain_ref, router_ref, picks_ref,
                   current_ref, rows_ref, weights_ref):
    tokens, width = current_ref.shape
    experts = router_ref.shape[0]
    picked = arrived_ref[...]
    current = jnp.where(first_ref[0] == 1, fresh_ref[...], picked)
    current_ref[...] = current
    values = current.astype(jnp.float32)
    inv_scale = lax.rsqrt(jnp.mean(values * values, axis=1, keepdims=True) + 1e-06)
    normed = (values * inv_scale * gain_ref[...]).astype(jnp.bfloat16)
    logits = dot(router_ref[...], normed, 1, 1)
    expert_ids = lax.broadcasted_iota(jnp.int32, (experts, tokens), 0)
    chosen = jnp.zeros((experts, tokens), jnp.float32)
    for choice in range(picks_ref.shape[0]):
        chosen = chosen + jnp.where(picks_ref[choice, step : step + 1, :] == expert_ids, 1.0, 0.0)
    scores = chosen / (1.0 + jnp.exp(-logits))
    mixing = scores / jnp.sum(scores, axis=0, keepdims=True)
    before = jnp.where(
        lax.broadcasted_iota(jnp.int32, (tokens, tokens), 0)
        < lax.broadcasted_iota(jnp.int32, (tokens, tokens), 1), 1.0, 0.0
    ).astype(jnp.bfloat16)
    rank = dot(chosen.astype(jnp.bfloat16), before)
    slot = jnp.where(chosen > 0.0, rank, float(CAP))
    slot_rows = jnp.broadcast_to(slot[:, None, :], (experts, CAP, tokens))
    slot_ids = lax.broadcasted_iota(jnp.int32, (experts, CAP, tokens), 1).astype(jnp.float32)
    here = slot_rows == slot_ids
    pick = jnp.where(here, 1.0, 0.0).reshape(experts * CAP, tokens).astype(jnp.bfloat16)
    mixed = jnp.where(here, jnp.broadcast_to(mixing[:, None, :], here.shape), 0.0)
    weights_ref[...] = mixed.reshape(experts * CAP, tokens).astype(jnp.bfloat16)
    for cols in column_tiles(width, 512):
        rows_ref[:, cols] = dot(pick, normed[:, cols]).astype(jnp.bfloat16)


def prepare(step, first, arrived, fresh, gain, router, picks):
    tokens, width = arrived.shape
    slots = router.shape[0] * CAP
    vmem = pl.BlockSpec(memory_space=pltpu.VMEM)
    return pl.pallas_call(
        lambda *refs: prepare_kernel(step, *refs),
        out_shape=(
            jax.ShapeDtypeStruct((tokens, width), jnp.bfloat16),
            jax.ShapeDtypeStruct((slots, width), jnp.bfloat16),
            jax.ShapeDtypeStruct((slots, tokens), jnp.bfloat16),
        ),
        in_specs=[pl.BlockSpec(memory_space=pltpu.SMEM)] + [vmem] * 5,
        out_specs=(vmem, vmem, vmem),
        name="prepare",
    )(first, arrived, fresh, gain, router, picks)


def experts_kernel(rows_ref, gate_hbm, up_hbm, down_hbm, out_ref, gate_ref, up_ref, down_ref, hidden_ref, arrived):
    width, inner = gate_ref.shape
    tiles = column_tiles(inner, 256)
    copies = []
    for index, cols in enumerate(tiles):
        for which, (source, target) in enumerate(((gate_hbm, gate_ref), (up_hbm, up_ref))):
            copies.append(pltpu.make_async_copy(source.at[:, cols], target.at[:, cols], arrived.at[2 * index + which]))
    last = pltpu.make_async_copy(down_hbm, down_ref, arrived.at[2 * len(tiles)])
    for copy in copies:
        copy.start()
    last.start()
    for index, cols in enumerate(tiles):
        copies[2 * index].wait()
        gate = dot(rows_ref[...], gate_ref[:, cols])
        copies[2 * index + 1].wait()
        up = dot(rows_ref[...], up_ref[:, cols])
        hidden_ref[:, cols] = (gate / (1.0 + jnp.exp(-gate)) * up).astype(jnp.bfloat16)
    last.wait()
    for cols in column_tiles(width, 512):
        out_ref[:, cols] = dot(hidden_ref[...], down_ref[:, cols]).astype(jnp.bfloat16)


def run_experts(rows, w_gate, w_up, w_down):
    count, width = rows.shape
    hidden = w_gate.shape[1]
    vmem, hbm = pl.BlockSpec(memory_space=pltpu.VMEM), pl.BlockSpec(memory_space=pl.ANY)
    return pl.pallas_call(
        experts_kernel,
        out_shape=jax.ShapeDtypeStruct((count, width), jnp.bfloat16),
        in_specs=[vmem, hbm, hbm, hbm],
        out_specs=vmem,
        scratch_shapes=[
            pltpu.VMEM((width, hidden), jnp.bfloat16),
            pltpu.VMEM((width, hidden), jnp.bfloat16),
            pltpu.VMEM((hidden, width), jnp.bfloat16),
            pltpu.VMEM((count, hidden), jnp.bfloat16),
            pltpu.SemaphoreType.DMA((2 * len(column_tiles(hidden, 256)) + 1,)),
        ],
        compiler_params=pltpu.CompilerParams(vmem_limit_bytes=40 << 20),
        name="experts",
    )(rows, w_gate, w_up, w_down)


def combine_kernel(earlier, current_ref, weights_ref, landed_ref, *refs):
    out_ref = refs[-1]
    weights = jnp.transpose(weights_ref[...])
    for index in range(earlier):
        out_ref[index] = refs[index][0]
    for cols in column_tiles(out_ref.shape[2], 512):
        total = current_ref[:, cols].astype(jnp.float32) + dot(weights, landed_ref[:, cols])
        out_ref[earlier, :, cols] = total.astype(jnp.bfloat16)


def combine(current, weights, landed, *results):
    vmem = pl.BlockSpec(memory_space=pltpu.VMEM)
    return pl.pallas_call(
        lambda *refs: combine_kernel(len(results), *refs),
        out_shape=jax.ShapeDtypeStruct((len(results) + 1, *current.shape), jnp.bfloat16),
        in_specs=[vmem] * (3 + len(results)),
        out_specs=vmem,
        name="combine",
    )(current, weights, landed, *results)


def exchange(rows):
    count, width = rows.shape
    parts = rows.reshape(count // CAP, CAP, width)
    moved = lax.all_to_all(parts, GROUP, split_axis=0, concat_axis=0, tiled=True)
    return moved.reshape(count, width)


def shards(entering, fresh, w_gate, w_up, w_down, router, gain, routes):
    at_start = (lax.axis_index("segment") == 0).astype(jnp.int32).reshape(1)
    never = jnp.zeros((1,), jnp.int32)
    router_rows = jnp.transpose(router[0])
    picks = jnp.transpose(routes[0], (2, 0, 1))
    w_gate, w_up, w_down = (
        pltpu.with_memory_space_constraint(value[0, 0], pltpu.HBM) for value in (w_gate, w_up, w_down)
    )
    results = []
    count = lax.axis_size("segment")
    steps = routes.shape[1]
    for step in range(steps):
        if step == 0:
            first, arrived, other = never, entering[0], entering[0]
        else:
            arrived = lax.ppermute(results[-1][0], "segment", [(i, i + 1) for i in range(count - 1)])
            first, other = at_start, fresh[step - 1]
        current, rows, weights = prepare(step, first, arrived, other, gain, router_rows, picks)
        landed = exchange(run_experts(exchange(rows), w_gate, w_up, w_down))
        results.append(combine(current, weights, landed, *(results if step == steps - 1 else [])))
    return results[-1][None]


def solution(mesh):
    tokens = P("segment", ("expert", "dp"), None)
    weights = P("segment", ("expert", "dp"), None, None)
    in_specs = (
        tokens, P(None, ("expert", "dp"), None), weights, weights, weights,
        P("segment", None, None), P("segment", None), P("segment", None, ("expert", "dp"), None),
    )
    out_specs = P("segment", None, ("expert", "dp"), None)
    return jax.shard_map(shards, mesh=mesh, in_specs=in_specs, out_specs=out_specs, check_vma=False)
```

time: 333 us -> 332 us (level)
  Pallas kernels: 32 us -> 39.5 us
  local copies, waits for them, and re-layouts: 6.26 us -> 0.72 us
    pallas_call x2, Pallas kernels: 17.8 us -> 25.1 us  [run_experts(): pl.pallas_call(experts_kernel, out_shape=jax.ShapeDtypeStruct((count, wid...]
    unnamed x13 -> x2, local copies, waits for them, and re-layouts: 5.65 us -> 0.72 us
where the time goes in v3:
time: 332 us
  blocking collectives  280 us (84%)
  Pallas kernels  39.5 us (12%)
  waiting for transfers between devices  9.75 us (3%)
    all_to_all x4, blocking collectives, exchange(): lax.all_to_all(parts, GROUP, split_axis=0, concat_axis=0, tiled=True)  280 us
    pallas_call x2, Pallas kernels, run_experts(): pl.pallas_call(experts_kernel, out_shape=jax.ShapeDtypeStruct((count, wid...  25.1 us
    ppermute x1, waiting for transfers between devices, shards(): lax.ppermute(results[-1][0], 'segment', [(i, i + 1) for i in range(count...  9.75 us
    pallas_call x2, Pallas kernels, prepare(): pl.pallas_call(lambda *refs: prepare_kernel(step, *refs), out_shape=(jax....  7.75 us
  transfers between devices with their start and end apart: 1, of which 1 were waited for; matrix products, arithmetic and copies ran while one was open for 0% of the time, Pallas kernels for 0%

profile of v3, /device:TPU:7, one launch (start us, length us, event | category | flops | bytes accessed | tf_op | source)
XLA Modules:
  0.0 331.7 jit_solution(14717020381953816374)
XLA Ops:
  0.0 3.9 %prepare.2 = (bf16[64,2560]{1,0:T(8,128)(2,1)}, bf16[512,2560]{1,0:T(8,128)(2,1)}, bf16[512,64]{1,0:T(8,128)(2,1)}) custom-call(s32[1]{0:T(128)} %constant.9.clone.1.refs_0_, bf16[64,2560]{1,0:T(8,128)(2,1)} %bitcast.36, bf16[64,2560]{1,0:T(8,128)(2,1)} %bitcast.37, f32[1,2560]{1,0:T(1,128)} %refs_3_.3, bf16[64,2560]{1,0:T(8,128)(2,1)} %bitcast.38, ...), custom_call_target="tpu_custom_call" | custom-call | tf_op jit(solution)/shard_map/prepare/pallas_call | solution.py:59
  3.9 75.0 %all_to_all.20 = bf16[64,8,2560]{2,1,0:T(8,128)(2,1)S(1)} all-to-all(bf16[64,8,2560]{2,1,0:T(8,128)(2,1)} %bitcast.35), channel_id=1, replica_groups=mesh['segment'=4,'expert'=32,'dp'=2] {'expert','dp'}, dimensions={0} | all-to-all | bytes 5242880 | tf_op jit(solution)/shard_map/all_to_all | solution.py:139
  78.9 12.6 %experts.2 = bf16[512,2560]{1,0:T(8,128)(2,1)S(1)} custom-call(bf16[512,2560]{1,0:T(8,128)(2,1)S(1)} %bitcast.22, bf16[2560,768]{1,0:T(8,128)(2,1)} %bitcast.26, bf16[2560,768]{1,0:T(8,128)(2,1)} %bitcast.28, bf16[768,2560]{1,0:T(8,128)(2,1)} %bitcast.30), custom_call_target="tpu_custom_call" | custom-call | tf_op jit(solution)/shard_map/experts/pallas_call | solution.py:98
  91.5 68.3 %all_to_all.21 = bf16[64,8,2560]{2,1,0:T(8,128)(2,1)} all-to-all(bf16[64,8,2560]{2,1,0:T(8,128)(2,1)S(1)} %bitcast.23), channel_id=1, replica_groups=mesh['segment'=4,'expert'=32,'dp'=2] {'expert','dp'}, dimensions={0} | all-to-all | bytes 5242880 | tf_op jit(solution)/shard_map/all_to_all | solution.py:139
  159.8 3.2 combine.2.refs_3_
  163.0 1.3 collective-permute-start
  164.3 9.7 %collective-permute-done.refs_1_ = bf16[64,2560]{1,0:T(8,128)(2,1)S(1)} collective-permute-done((bf16[64,2560]{1,0:T(8,128)(2,1)}, bf16[64,2560]{1,0:T(8,128)(2,1)S(1)}, u32[]{:S(2)}, u32[]{:S(2)}) %collective-permute-start) | collective-permute-done | bytes 327712 | tf_op jit(solution)/shard_map/ppermute | solution.py:158
  174.1 0.0 copy-start
  174.1 0.7 copy-done
  174.8 3.9 %prepare.3 = (bf16[64,2560]{1,0:T(8,128)(2,1)}, bf16[512,2560]{1,0:T(8,128)(2,1)}, bf16[512,64]{1,0:T(8,128)(2,1)}) custom-call(s32[1]{0:T(128)} %bitcast.refs_0_, bf16[64,2560]{1,0:T(8,128)(2,1)} %copy-done, bf16[64,2560]{1,0:T(8,128)(2,1)} %bitcast.41, f32[1,2560]{1,0:T(1,128)} %refs_3_.3, bf16[64,2560]{1,0:T(8,128)(2,1)} %bitcast.39, s32[6,2,64]{2,1,0:T(2,128)} %bitcast.43), custom_call_target="tpu_custom_call" | custom-call | tf_op jit(solution)/shard_map/prepare/pallas_call | solution.py:59
  178.7 68.8 %all_to_all.22 = bf16[64,8,2560]{2,1,0:T(8,128)(2,1)S(1)} all-to-all(bf16[64,8,2560]{2,1,0:T(8,128)(2,1)} %bitcast.34), channel_id=1, replica_groups=mesh['segment'=4,'expert'=32,'dp'=2] {'expert','dp'}, dimensions={0} | all-to-all | bytes 5242880 | tf_op jit(solution)/shard_map/all_to_all | solution.py:139
  247.4 12.6 %experts.3 = bf16[512,2560]{1,0:T(8,128)(2,1)S(1)} custom-call(bf16[512,2560]{1,0:T(8,128)(2,1)S(1)} %bitcast.24, bf16[2560,768]{1,0:T(8,128)(2,1)} %bitcast.27, bf16[2560,768]{1,0:T(8,128)(2,1)} %bitcast.29, bf16[768,2560]{1,0:T(8,128)(2,1)} %bitcast.31), custom_call_target="tpu_custom_call" | custom-call | tf_op jit(solution)/shard_map/experts/pallas_call | solution.py:98
  260.0 68.3 %all_to_all.23 = bf16[64,8,2560]{2,1,0:T(8,128)(2,1)} all-to-all(bf16[64,8,2560]{2,1,0:T(8,128)(2,1)S(1)} %bitcast.25), channel_id=1, replica_groups=mesh['segment'=4,'expert'=32,'dp'=2] {'expert','dp'}, dimensions={0} | all-to-all | bytes 5242880 | tf_op jit(solution)/shard_map/all_to_all | solution.py:139
  328.3 3.4 %combine.3 = bf16[2,64,2560]{2,1,0:T(8,128)(2,1)} custom-call(bf16[64,2560]{1,0:T(8,128)(2,1)} %get-tuple-element.14.refs_0_, bf16[512,64]{1,0:T(8,128)(2,1)} %get-tuple-element.15.refs_1_, bf16[512,2560]{1,0:T(8,128)(2,1)} %bitcast.32, bf16[1,64,2560]{2,1,0:T(8,128)(2,1)} %combine.2.refs_3_), custom_call_target="tpu_custom_call" | custom-call | tf_op jit(solution)/shard_map/combine/pallas_call | solution.py:127
Async XLA Ops:
  163.0 11.0 %collective-permute-start = (bf16[64,2560]{1,0:T(8,128)(2,1)}, bf16[64,2560]{1,0:T(8,128)(2,1)S(1)}, u32[]{:S(2)}, u32[]{:S(2)}) collective-permute-start(bf16[64,2560]{1,0:T(8,128)(2,1)} %bitcast.40), channel_id=1, source_target_pairs={{0,64},{64,128},{128,192},{1,65},{65,129},{129,193},{2,66},{66,130... | collective-permute-start | bytes 983048 | tf_op jit(solution)/shard_map/ppermute | solution.py:158
  174.1 0.7 copy-start

commit v4 on v3

--- a/solution.py
+++ b/solution.py
@@ -69,26 +69,34 @@
     )(first, arrived, fresh, gain, router, picks)
 
 
-def experts_kernel(rows_ref, gate_hbm, up_hbm, down_hbm, out_ref, gate_ref, up_ref, down_ref, hidden_ref, arrived):
+def experts_kernel(rows_ref, gate_hbm, up_hbm, down_hbm, out_ref,
+                   gate_ref, up_ref, down_ref, gated_ref, upper_ref, hidden_ref, arrived):
     width, inner = gate_ref.shape
-    tiles = column_tiles(inner, 256)
+    parts, tiles = column_tiles(width, 512), column_tiles(inner, 256)
     copies = []
-    for index, cols in enumerate(tiles):
+    for index, part in enumerate(parts):
         for which, (source, target) in enumerate(((gate_hbm, gate_ref), (up_hbm, up_ref))):
-            copies.append(pltpu.make_async_copy(source.at[:, cols], target.at[:, cols], arrived.at[2 * index + which]))
-    last = pltpu.make_async_copy(down_hbm, down_ref, arrived.at[2 * len(tiles)])
+            copies.append(pltpu.make_async_copy(source.at[part, :], target.at[part, :], arrived.at[2 * index + which]))
+    last = pltpu.make_async_copy(down_hbm, down_ref, arrived.at[2 * len(parts)])
     for copy in copies:
         copy.start()
     last.start()
-    for index, cols in enumerate(tiles):
+    for index, part in enumerate(parts):
         copies[2 * index].wait()
-        gate = dot(rows_ref[...], gate_ref[:, cols])
         copies[2 * index + 1].wait()
-        up = dot(rows_ref[...], up_ref[:, cols])
-        hidden_ref[:, cols] = (gate / (1.0 + jnp.exp(-gate)) * up).astype(jnp.bfloat16)
+        rows = rows_ref[:, part]
+        for cols in tiles:
+            gate, up = dot(rows, gate_ref[part, cols]), dot(rows, up_ref[part, cols])
+            if index > 0:
+                gate, up = gated_ref[:, cols] + gate, upper_ref[:, cols] + up
+            if index < len(parts) - 1:
+                gated_ref[:, cols], upper_ref[:, cols] = gate, up
+            else:
+                hidden_ref[:, cols] = (gate / (1.0 + jnp.exp(-gate)) * up).astype(jnp.bfloat16)
     last.wait()
+    hidden = hidden_ref[...]
     for cols in column_tiles(width, 512):
-        out_ref[:, cols] = dot(hidden_ref[...], down_ref[:, cols]).astype(jnp.bfloat16)
+        out_ref[:, cols] = dot(hidden, down_ref[:, cols]).astype(jnp.bfloat16)
 
 
 def run_experts(rows, w_gate, w_up, w_down):
@@ -104,10 +112,12 @@
             pltpu.VMEM((width, hidden), jnp.bfloat16),
             pltpu.VMEM((width, hidden), jnp.bfloat16),
             pltpu.VMEM((hidden, width), jnp.bfloat16),
+            pltpu.VMEM((count, hidden), jnp.float32),
+            pltpu.VMEM((count, hidden), jnp.float32),
             pltpu.VMEM((count, hidden), jnp.bfloat16),
-            pltpu.SemaphoreType.DMA((2 * len(column_tiles(hidden, 256)) + 1,)),
+            pltpu.SemaphoreType.DMA((2 * len(column_tiles(width, 512)) + 1,)),
         ],
-        compiler_params=pltpu.CompilerParams(vmem_limit_bytes=40 << 20),
+        compiler_params=pltpu.CompilerParams(vmem_limit_bytes=44 << 20),
         name="experts",
     )(rows, w_gate, w_up, w_down)
 

time: 332 us -> 324 us (0.976)
  Pallas kernels: 39.5 us -> 31.3 us
    pallas_call x2, Pallas kernels: 25.1 us -> 17 us  [run_experts(): pl.pallas_call(experts_kernel, out_shape=jax.ShapeDtypeStruct((count, wid...]
where the time goes in v4:
time: 324 us
  blocking collectives  280 us (86%)
  Pallas kernels  31.3 us (10%)
  waiting for transfers between devices  9.76 us (3%)
    all_to_all x4, blocking collectives, exchange(): lax.all_to_all(parts, GROUP, split_axis=0, concat_axis=0, tiled=True)  280 us
    pallas_call x2, Pallas kernels, run_experts(): pl.pallas_call(experts_kernel, out_shape=jax.ShapeDtypeStruct((count, wid...  17 us
    ppermute x1, waiting for transfers between devices, shards(): lax.ppermute(results[-1][0], 'segment', [(i, i + 1) for i in range(count...  9.76 us
    pallas_call x2, Pallas kernels, prepare(): pl.pallas_call(lambda *refs: prepare_kernel(step, *refs), out_shape=(jax....  7.75 us
    pallas_call x2, Pallas kernels, combine(): pl.pallas_call(lambda *refs: combine_kernel(len(results), *refs), out_sha...  6.61 us
  transfers between devices with their start and end apart: 1, of which 1 were waited for; matrix products, arithmetic and copies ran while one was open for 0% of the time, Pallas kernels for 0%

profile of v4, /device:TPU:7, one launch (start us, length us, event | category | flops | bytes accessed | tf_op | source)
XLA Modules:
  0.0 323.5 jit_solution(8459737378427480097)
XLA Ops:
  0.0 3.9 %prepare.2 = (bf16[64,2560]{1,0:T(8,128)(2,1)}, bf16[512,2560]{1,0:T(8,128)(2,1)}, bf16[512,64]{1,0:T(8,128)(2,1)}) custom-call(s32[1]{0:T(128)} %constant.9.clone.1.refs_0_, bf16[64,2560]{1,0:T(8,128)(2,1)} %bitcast.36, bf16[64,2560]{1,0:T(8,128)(2,1)} %bitcast.37, f32[1,2560]{1,0:T(1,128)} %refs_3_.3, bf16[64,2560]{1,0:T(8,128)(2,1)} %bitcast.38, ...), custom_call_target="tpu_custom_call" | custom-call | tf_op jit(solution)/shard_map/prepare/pallas_call | solution.py:59
  3.9 75.0 %all_to_all.20 = bf16[64,8,2560]{2,1,0:T(8,128)(2,1)S(1)} all-to-all(bf16[64,8,2560]{2,1,0:T(8,128)(2,1)} %bitcast.35), channel_id=1, replica_groups=mesh['segment'=4,'expert'=32,'dp'=2] {'expert','dp'}, dimensions={0} | all-to-all | bytes 5242880 | tf_op jit(solution)/shard_map/all_to_all | solution.py:149
  78.9 8.5 %experts.2 = bf16[512,2560]{1,0:T(8,128)(2,1)S(1)} custom-call(bf16[512,2560]{1,0:T(8,128)(2,1)S(1)} %bitcast.22, bf16[2560,768]{1,0:T(8,128)(2,1)} %bitcast.26, bf16[2560,768]{1,0:T(8,128)(2,1)} %bitcast.28, bf16[768,2560]{1,0:T(8,128)(2,1)} %bitcast.30), custom_call_target="tpu_custom_call" | custom-call | tf_op jit(solution)/shard_map/experts/pallas_call | solution.py:106
  87.4 68.3 %all_to_all.21 = bf16[64,8,2560]{2,1,0:T(8,128)(2,1)} all-to-all(bf16[64,8,2560]{2,1,0:T(8,128)(2,1)S(1)} %bitcast.23), channel_id=1, replica_groups=mesh['segment'=4,'expert'=32,'dp'=2] {'expert','dp'}, dimensions={0} | all-to-all | bytes 5242880 | tf_op jit(solution)/shard_map/all_to_all | solution.py:149
  155.7 3.2 %combine.2.refs_3_ = bf16[1,64,2560]{2,1,0:T(8,128)(2,1)} custom-call(bf16[64,2560]{1,0:T(8,128)(2,1)} %get-tuple-element.11.refs_0_, bf16[512,64]{1,0:T(8,128)(2,1)} %get-tuple-element.12.refs_1_, bf16[512,2560]{1,0:T(8,128)(2,1)} %bitcast.33), custom_call_target="tpu_custom_call" | custom-call | tf_op jit(solution)/shard_map/combine/pallas_call | solution.py:137
  158.9 1.3 collective-permute-start
  160.2 9.8 %collective-permute-done.refs_1_ = bf16[64,2560]{1,0:T(8,128)(2,1)S(1)} collective-permute-done((bf16[64,2560]{1,0:T(8,128)(2,1)}, bf16[64,2560]{1,0:T(8,128)(2,1)S(1)}, u32[]{:S(2)}, u32[]{:S(2)}) %collective-permute-start) | collective-permute-done | bytes 327712 | tf_op jit(solution)/shard_map/ppermute | solution.py:168
  170.0 0.0 copy-start
  170.0 0.7 copy-done
  170.7 3.9 %prepare.3 = (bf16[64,2560]{1,0:T(8,128)(2,1)}, bf16[512,2560]{1,0:T(8,128)(2,1)}, bf16[512,64]{1,0:T(8,128)(2,1)}) custom-call(s32[1]{0:T(128)} %bitcast.refs_0_, bf16[64,2560]{1,0:T(8,128)(2,1)} %copy-done, bf16[64,2560]{1,0:T(8,128)(2,1)} %bitcast.41, f32[1,2560]{1,0:T(1,128)} %refs_3_.3, bf16[64,2560]{1,0:T(8,128)(2,1)} %bitcast.39, s32[6,2,64]{2,1,0:T(2,128)} %bitcast.43), custom_call_target="tpu_custom_call" | custom-call | tf_op jit(solution)/shard_map/prepare/pallas_call | solution.py:59
  174.6 68.7 %all_to_all.22 = bf16[64,8,2560]{2,1,0:T(8,128)(2,1)S(1)} all-to-all(bf16[64,8,2560]{2,1,0:T(8,128)(2,1)} %bitcast.34), channel_id=1, replica_groups=mesh['segment'=4,'expert'=32,'dp'=2] {'expert','dp'}, dimensions={0} | all-to-all | bytes 5242880 | tf_op jit(solution)/shard_map/all_to_all | solution.py:149
  243.3 8.5 %experts.3 = bf16[512,2560]{1,0:T(8,128)(2,1)S(1)} custom-call(bf16[512,2560]{1,0:T(8,128)(2,1)S(1)} %bitcast.24, bf16[2560,768]{1,0:T(8,128)(2,1)} %bitcast.27, bf16[2560,768]{1,0:T(8,128)(2,1)} %bitcast.29, bf16[768,2560]{1,0:T(8,128)(2,1)} %bitcast.31), custom_call_target="tpu_custom_call" | custom-call | tf_op jit(solution)/shard_map/experts/pallas_call | solution.py:106
  251.9 68.3 %all_to_all.23 = bf16[64,8,2560]{2,1,0:T(8,128)(2,1)} all-to-all(bf16[64,8,2560]{2,1,0:T(8,128)(2,1)S(1)} %bitcast.25), channel_id=1, replica_groups=mesh['segment'=4,'expert'=32,'dp'=2] {'expert','dp'}, dimensions={0} | all-to-all | bytes 5242880 | tf_op jit(solution)/shard_map/all_to_all | solution.py:149
  320.1 3.4 %combine.3 = bf16[2,64,2560]{2,1,0:T(8,128)(2,1)} custom-call(bf16[64,2560]{1,0:T(8,128)(2,1)} %get-tuple-element.14.refs_0_, bf16[512,64]{1,0:T(8,128)(2,1)} %get-tuple-element.15.refs_1_, bf16[512,2560]{1,0:T(8,128)(2,1)} %bitcast.32, bf16[1,64,2560]{2,1,0:T(8,128)(2,1)} %combine.2.refs_3_), custom_call_target="tpu_custom_call" | custom-call | tf_op jit(solution)/shard_map/combine/pallas_call | solution.py:137
Async XLA Ops:
  158.9 11.1 %collective-permute-start = (bf16[64,2560]{1,0:T(8,128)(2,1)}, bf16[64,2560]{1,0:T(8,128)(2,1)S(1)}, u32[]{:S(2)}, u32[]{:S(2)}) collective-permute-start(bf16[64,2560]{1,0:T(8,128)(2,1)} %bitcast.40), channel_id=1, source_target_pairs={{0,64},{64,128},{128,192},{1,65},{65,129},{129,193},{2,66},{66,130... | collective-permute-start | bytes 983048 | tf_op jit(solution)/shard_map/ppermute | solution.py:168
  170.0 0.7 copy-start
